TPU v7x, 32 devices: a whole 2x2x4 slice. The times are simulated.
32 devices in a mesh: aux: 4 (over y, x), row: 4 (over z), col: 2 (over core).
Axes of the slice: x: 2, y: 2, z: 4, core: 2. Of those that a mesh axis runs over, the one named last changes fastest.
Arguments:
- integrals: bfloat16 [2560, 64, 4096], P('aux', ('row', 'col')), may hold values from -6 to 6
- pair_blocks: int32 [2, 64], P(None, ('row', 'col')), may hold values from -1 to 15, as said below
- occupied: bfloat16 [1024, 64], P('col'), may hold values from -0.75 to 0.75
- metric: bfloat16 [2560, 2560], replicated, as said below
Outputs:
- exchange_k: float32 [1024, 1024], P('row', ('aux', 'col'))
Inputs may be any that keep to these rules, and one draw needn't show every extreme that they name: `pair_blocks`: A slot of row group r and column group c (slots (r * number of column groups + c) * 8 onward) is empty (-1 in both entries) or names a row block of r's 4 blocks and a column block of c's 8 blocks; no block pair is named twice; live slots of a group come before its empty ones; every group has 4 or more live slots and some group has all 8 live. `metric`: symmetric.
All inputs are finite; a program needn't handle non-finite values.
Results may differ from a plain program's by a relative error of at most 0.0003.
Values sent between devices are 32-bit elements; how exact they have to be, the bound alone decides.
A program may use at most 256 MiB of HBM per device.

v0:
```python
import functools

import jax
import jax.numpy as jnp
from jax import lax
from jax.experimental import pallas as pl
from jax.experimental.pallas import tpu as pltpu
from jax.sharding import PartitionSpec as P

BS = 64
OCT = 8
EIGHTHS = (1, 2, 4, 1)
QT = 512
VMEM_LIMIT = 60 * 1024 * 1024


def gathered_plan(integrals, pair_blocks, occupied, metric, nbf):
    aux_rows, slot_count = integrals.shape[:2]
    occ_count = occupied.shape[1]
    rows_local = nbf // lax.axis_size("row")
    row_blocks = rows_local // BS
    metric_wide = metric.astype(jnp.float32)

    def add_slot(carry, slot):
        row_block = pair_blocks[0, slot]
        col_block = pair_blocks[1, slot]
        local_row = jnp.maximum(row_block, 0) % row_blocks
        local_col = jnp.maximum(col_block, 0) % (occupied.shape[0] // BS)
        tile = lax.dynamic_index_in_dim(integrals, slot, 1, False).reshape(aux_rows, BS, BS)
        cpart = lax.dynamic_slice_in_dim(occupied, local_col * BS, BS, 0)
        piece = jnp.einsum("pmn,ni->ipm", tile, cpart, preferred_element_type=jnp.float32)
        piece = jnp.where(row_block >= 0, piece, 0.0)
        current = lax.dynamic_slice_in_dim(carry, local_row * BS, BS, 2)
        return lax.dynamic_update_slice_in_dim(carry, current + piece, local_row * BS, 2), None

    start = jnp.zeros((occ_count, aux_rows, rows_local), jnp.float32)
    partials, _ = lax.scan(add_slot, start, jnp.arange(slot_count, dtype=jnp.int32))
    summed = lax.psum_scatter(partials, "col", scatter_dimension=1, tiled=True)
    half = lax.all_to_all(summed, ("aux", "col"), split_axis=0, concat_axis=1, tiled=True)
    highest = dict(precision=lax.Precision.HIGHEST, preferred_element_type=jnp.float32)
    fitted = jnp.einsum("qp,ipm->iqm", metric_wide, half, **highest)
    contrib = jnp.einsum("iqm,iqn->mn", fitted, lax.all_gather(fitted, "row", axis=2, tiled=True), **highest)
    return lax.psum_scatter(contrib, ("aux", "col"), scatter_dimension=1, tiled=True)


def contract_kernel(info_ref, occ_ref, x_ref, other_ref, mine_ref, xt_ref, w_ref):
    slots = x_ref.shape[1]
    half, _, octet, aux_rows = mine_ref.shape
    occ = 2 * half
    tall, wide = occ * octet, octet * BS
    f32 = dict(preferred_element_type=jnp.float32)

    @pl.when(pl.program_id(0) == 0)
    def _():
        spread = lax.broadcasted_iota(jnp.int32, (tall, occ), 0) // octet == lax.broadcasted_iota(
            jnp.int32, (tall, occ), 1
        )
        spread = spread.astype(jnp.bfloat16)
        tile = lax.broadcasted_iota(jnp.int32, (BS, wide), 1) % BS == lax.broadcasted_iota(jnp.int32, (BS, wide), 0)
        tile = tile.astype(jnp.bfloat16)
        keep = (
            lax.broadcasted_iota(jnp.int32, (tall, wide), 0) % octet
            == lax.broadcasted_iota(jnp.int32, (tall, wide), 1) // BS
        )

        def build(s, _):
            live = info_ref[1 + 2 * slots + s] > 0
            start = pl.multiple_of(info_ref[1 + slots + s] * BS, BS)
            coeffs = occ_ref[pl.ds(start, BS), :]
            rows = lax.dot_general(spread, coeffs, (((1,), (1,)), ((), ())), **f32).astype(jnp.bfloat16)
            full = jnp.dot(rows, tile, **f32)
            w_ref[s] = jnp.where(jnp.logical_and(keep, live), full, 0.0).astype(jnp.bfloat16)
            return 0

        lax.fori_loop(0, slots, build, 0)

    def turn(q, _):
        at = pl.ds(pl.multiple_of(q * 128, 128), 128)
        xt_ref[:, at] = pltpu.einshape("psk->spk", x_ref[at].astype(jnp.float32)).astype(jnp.bfloat16)
        return 0

    lax.fori_loop(0, aux_rows // 128, turn, 0)
    col = info_ref[0]
    for h, out_ref in ((1 - col, other_ref), (col, mine_ref)):
        out_ref[...] = jnp.zeros_like(out_ref)

        def one(s, _):
            w = w_ref[s, pl.ds(pl.multiple_of(h * half * octet, 16), half * octet)]
            piece = lax.dot_general(w, xt_ref[s], (((1,), (1,)), ((), ())), **f32)
            b = info_ref[1 + s]
            out_ref[:, b] = out_ref[:, b] + piece.reshape(half, octet, aux_rows)
            return 0

        lax.fori_loop(0, slots, one, 0)


def contract(info, occupied, integrals, lo, m, row_blocks):
    aux_rows, slots, _ = integrals.shape
    rows_in, occ = occupied.shape
    out = jax.ShapeDtypeStruct((occ // 2, row_blocks, m, aux_rows), jnp.float32)
    spec = pl.BlockSpec((occ // 2, row_blocks, OCT, aux_rows), lambda j, info: (0, 0, j, 0))
    return pl.pallas_call(
        contract_kernel,
        grid_spec=pltpu.PrefetchScalarGridSpec(
            num_scalar_prefetch=1,
            grid=(m // OCT,),
            in_specs=[
                pl.BlockSpec((rows_in, occ), lambda j, info: (0, 0)),
                pl.BlockSpec((aux_rows, slots, OCT * BS), lambda j, info: (0, 0, j + lo // OCT)),
            ],
            out_specs=[spec, spec],
            scratch_shapes=[
                pltpu.VMEM((slots, aux_rows, OCT * BS), jnp.bfloat16),
                pltpu.VMEM((slots, occ * OCT, OCT * BS), jnp.bfloat16),
            ],
        ),
        out_shape=[out, out],
        compiler_params=pltpu.CompilerParams(vmem_limit_bytes=VMEM_LIMIT),
        cost_estimate=pl.CostEstimate(
            flops=2 * slots * aux_rows * occ * OCT * m * BS,
            bytes_accessed=2 * slots * aux_rows * m * BS + 4 * occ * row_blocks * m * aux_rows,
            transcendentals=0,
        ),
        name="contract",
    )(info, occupied, integrals)


def combine_kernel(me_ref, mine_ref, got_ref, *out_refs):
    me = me_ref[0]
    for d, out_ref in enumerate(out_refs):
        dest = lax.bitwise_xor(me, d)
        out_ref[...] = mine_ref[dest] + got_ref[dest]


def combine(me, mine, got):
    group, share, rows, aux_rows = mine.shape
    piece = jax.ShapeDtypeStruct((share, rows, aux_rows), jnp.float32)
    vmem = pl.BlockSpec(memory_space=pltpu.VMEM)
    return pl.pallas_call(
        combine_kernel,
        in_specs=[pl.BlockSpec(memory_space=pltpu.SMEM), vmem, vmem],
        out_specs=[vmem] * group,
        out_shape=[piece] * group,
        compiler_params=pltpu.CompilerParams(vmem_limit_bytes=VMEM_LIMIT),
        cost_estimate=pl.CostEstimate(flops=mine.size, bytes_accessed=12 * mine.size, transcendentals=0),
        name="combine",
    )(me, mine, got)


def high_low(x):
    high = x.astype(jnp.bfloat16)
    return high, (x - high.astype(jnp.float32)).astype(jnp.bfloat16)


def consume_kernel(me_ref, *refs, n_row, starts, sizes, last):
    c = len(sizes) - 1
    refs = list(refs)
    n_pieces = len(refs) - 4 - 2 * c - (1 if c else 0) - (0 if last else 2)
    pieces, refs = refs[:n_pieces], refs[n_pieces:]
    m_ref, refs = refs[0], refs[1:]
    earlier, refs = refs[: 2 * c], refs[2 * c :]
    if c:
        k_in, refs = refs[0], refs[1:]
    if not last:
        fh_ref, fl_ref, refs = refs[0], refs[1], refs[2:]
    k_ref, h_ref, cross_ref = refs
    me = me_ref[0]
    share, rows, aux_rows = pieces[0].shape
    total = rows * n_row
    blocks = k_ref.shape[0]
    j = pl.program_id(0)

    @pl.when(j == 0)
    def _():
        if c:
            k_ref[...] = k_in[...]
        else:
            k_ref[...] = jnp.zeros_like(k_ref)
        cross_ref[...] = jnp.zeros_like(cross_ref)
        for d, piece in enumerate(pieces):
            source = lax.bitwise_xor(me, d)
            aux = lax.div(source, n_row)
            row = lax.rem(source, n_row)
            lanes = pl.ds(pl.multiple_of(aux * aux_rows, 128), aux_rows)
            for t in range(share):
                high, low = high_low(piece[t])
                at = pl.multiple_of(row * rows, 16)
                h_ref[pl.ds(at + t * total, rows), lanes] = high
                h_ref[pl.ds(at + (share + t) * total, rows), lanes] = low

    f32 = dict(preferred_element_type=jnp.float32)
    both = jnp.dot(h_ref[...], m_ref[...], **f32)
    fh, fl = high_low(both[: share * total] + both[share * total :])
    if not last:
        fh_ref[...] = fh.reshape(fh_ref.shape)
        fl_ref[...] = fl.reshape(fl_ref.shape)

    def outer(a, b):
        a, b = jnp.concatenate(a, 1), jnp.concatenate(b, 1)
        return lax.dot_general(a, b, (((1,), (1,)), ((), ())), **f32)

    def part(ci, cj):
        rows_at = pl.ds(starts[ci], sizes[ci])
        lanes_at = pl.ds(blocks * starts[cj], blocks * sizes[cj])
        return (slice(None), rows_at, lanes_at), (blocks, sizes[ci], blocks * sizes[cj])

    ah = [fh[t * total : (t + 1) * total] for t in range(share)]
    al = [fl[t * total : (t + 1) * total] for t in range(share)]
    at, shape = part(c, c)
    k_ref[at] = k_ref[at] + outer(ah, ah).reshape(shape)
    cross_ref[...] = cross_ref[...] + outer(ah, al)
    for e in range(c):
        bh = [earlier[2 * e][t] for t in range(share)]
        bl = [earlier[2 * e + 1][t] for t in range(share)]
        at, shape = part(c, e)
        k_ref[at] = k_ref[at] + outer(ah + ah + al, bh + bl + bh).reshape(shape)

    @pl.when(j == pl.num_programs(0) - 1)
    def _():
        at, shape = part(c, c)
        cross = cross_ref[...]
        k_ref[at] = k_ref[at] + (cross + cross.T).reshape(shape)
        for e in range(c):
            at, _ = part(c, e)
            turned = k_ref[at].reshape(total, -1).T
            at, shape = part(e, c)
            k_ref[at] = turned.reshape(shape)


def consume(me, pieces, metric, earlier, k_so_far, n_row, nbf, starts, sizes, last):
    share, rows, aux_rows = pieces[0].shape
    total = rows * n_row
    n_aux_all = metric.shape[0]
    once = pl.Buffered(1)
    whole = pl.BlockSpec((share, rows, aux_rows), lambda j: (0, 0, 0), pipeline_mode=once)
    in_specs = [pl.BlockSpec(memory_space=pltpu.SMEM)] + [whole] * len(pieces)
    in_specs.append(pl.BlockSpec((n_aux_all, QT), lambda j: (0, j)))
    in_specs += [pl.BlockSpec((f.shape[0], f.shape[1], QT), lambda j: (0, 0, j)) for f in earlier]
    k_shape = (nbf // BS, BS, nbf)
    k_spec = pl.BlockSpec(k_shape, lambda j: (0, 0, 0), pipeline_mode=once)
    args = [me, *pieces, metric, *earlier]
    if k_so_far is not None:
        in_specs.append(k_spec)
        args.append(k_so_far)
    out_specs, out_shape = [], []
    if not last:
        out_specs += [pl.BlockSpec((share, total, QT), lambda j: (0, 0, j))] * 2
        out_shape += [jax.ShapeDtypeStruct((share, total, n_aux_all), jnp.bfloat16)] * 2
    out_specs.append(k_spec)
    out_shape.append(jax.ShapeDtypeStruct(k_shape, jnp.float32))
    scratch = [pltpu.VMEM((2 * share * total, n_aux_all), jnp.bfloat16), pltpu.VMEM((total, total), jnp.float32)]
    done = nbf // BS * sum(sizes)
    return pl.pallas_call(
        functools.partial(consume_kernel, n_row=n_row, starts=starts, sizes=sizes, last=last),
        grid=(n_aux_all // QT,),
        in_specs=in_specs,
        out_specs=out_specs,
        out_shape=out_shape,
        scratch_shapes=scratch,
        compiler_params=pltpu.CompilerParams(vmem_limit_bytes=VMEM_LIMIT),
        cost_estimate=pl.CostEstimate(
            flops=4 * share * total * n_aux_all * n_aux_all + 6 * share * total * done * n_aux_all,
            bytes_accessed=2 * metric.size + 4 * share * total * n_aux_all,
            transcendentals=0,
        ),
        name="consume",
    )(*args)


def body(integrals, pair_blocks, occupied, metric, nbf):
    n_aux, n_row, n_col = lax.axis_size("aux"), lax.axis_size("row"), lax.axis_size("col")
    occ = occupied.shape[1]
    devices = n_aux * n_row * n_col
    group = n_aux * n_row
    aux_rows, _, _ = integrals.shape
    groups = n_aux * n_col
    fits = (
        n_col == 2
        and occ % devices == 0
        and aux_rows % 128 == 0
        and group & (group - 1) == 0
        and nbf % (groups * BS) == 0
        and nbf // BS * OCT % 128 == 0
        and metric.shape[0] % QT == 0
    )
    if not fits:
        return gathered_plan(integrals, pair_blocks, occupied, metric, nbf)
    row_blocks = nbf // n_row // BS
    share = occ // devices
    me = lax.axis_index("aux") * n_row + lax.axis_index("row")
    me_array = me.reshape(1).astype(jnp.int32)

    live = (pair_blocks[0] >= 0).astype(jnp.int32)
    rows = jnp.maximum(pair_blocks[0], 0) % row_blocks
    cols = jnp.maximum(pair_blocks[1], 0) % (occupied.shape[0] // BS)
    info = jnp.concatenate([lax.axis_index("col").reshape(1).astype(jnp.int32), rows, cols, live]).astype(jnp.int32)

    sizes = tuple(e * BS // 8 for e in EIGHTHS)
    starts = tuple(sum(sizes[:c]) for c in range(len(sizes)))
    arrived = []
    for lo, m in zip(starts, sizes):
        c = len(arrived)
        other, mine = contract(info, occupied, integrals, lo, m, row_blocks)
        got = lax.ppermute(other, "col", [(0, 1), (1, 0)])
        shape = (group, share, row_blocks * m, aux_rows)
        pieces = list(combine(me_array, mine.reshape(shape), got.reshape(shape)))
        info, me_array, pieces[0] = lax.optimization_barrier((info, me_array, pieces[0]))
        sent = [None] * group
        for d in sorted(range(group), key=lambda d: -bin(d).count("1")):
            pairs = [(s, s ^ d) for s in range(group)]
            sent[d] = pieces[d] if d == 0 else lax.ppermute(pieces[d], ("aux", "row"), pairs)
        arrived.append(sent)

    earlier, total = [], None
    for c in range(len(sizes)):
        last = c == len(sizes) - 1
        out = consume(me_array, arrived[c], metric, earlier, total, n_row, nbf, starts[: c + 1], sizes[: c + 1], last)
        total = out[-1]
        earlier += out[:-1]

    blocks = nbf // BS
    part = lax.psum_scatter(total, ("aux", "col"), scatter_dimension=0, tiled=True)
    part = part.reshape(-1, nbf).T
    strips = [part[blocks * lo : blocks * (lo + m)].reshape(blocks, m, -1) for lo, m in zip(starts, sizes)]
    part = jnp.concatenate(strips, 1).reshape(nbf, -1)
    return lax.psum_scatter(part, "row", scatter_dimension=0, tiled=True)


def solution(mesh):
    def local(*args, nbf):
        return body(*args, nbf)

    def whole(integrals, pair_blocks, occupied, metric):
        nbf = occupied.shape[0]
        return jax.shard_map(
            functools.partial(local, nbf=nbf),
            mesh=mesh,
            in_specs=(P("aux", ("row", "col"), None), P(None, ("row", "col")), P("col", None), P()),
            out_specs=P("row", ("aux", "col")),
            check_vma=False,
        )(integrals, pair_blocks, occupied, metric)

    return whole
```

profile of v0, /device:TPU:0, one launch (start us, length us, event | category | flops | bytes accessed | tf_op | source)
XLA Modules:
  0.0 793.2 jit_solution(17282068356101351097)
XLA Ops:
  10.2 18.5 %contract.4 = (f32[32,4,8,640]{3,2,1,0:T(8,128)}, f32[32,4,8,640]{3,2,1,0:T(8,128)}) custom-call(s32[25]{0:T(128)} %pad_add_fusion.info_ref, bf16[512,64]{1,0:T(8,128)(2,1)} %copy.13.occ_ref, bf16[640,8,4096]{2,1,0:T(8,128)(2,1)} %x_ref.7), custom_call_target="tpu_custom_call" | custom-call | flops 2684354560 | bytes 10485760 | tf_op jit(solution)/shard_map/contract/pallas_call | solution.py:102
  39.8 28.6 %contract.5 = (f32[32,4,16,640]{3,2,1,0:T(8,128)}, f32[32,4,16,640]{3,2,1,0:T(8,128)}) custom-call(s32[25]{0:T(128)} %pad_add_fusion.info_ref, bf16[512,64]{1,0:T(8,128)(2,1)} %copy.13.occ_ref, bf16[640,8,4096]{2,1,0:T(8,128)(2,1)} %x_ref.7), custom_call_target="tpu_custom_call" | custom-call | flops 5368709120 | bytes 20971520 | tf_op jit(solution)/shard_map/contract/pallas_call | solution.py:102
  84.5 48.3 %contract.6 = (f32[32,4,32,640]{3,2,1,0:T(8,128)}, f32[32,4,32,640]{3,2,1,0:T(8,128)}) custom-call(s32[25]{0:T(128)} %pad_add_fusion.info_ref, bf16[512,64]{1,0:T(8,128)(2,1)} %copy.13.occ_ref, bf16[640,8,4096]{2,1,0:T(8,128)(2,1)} %x_ref.7), custom_call_target="tpu_custom_call" | custom-call | flops 10737418240 | bytes 41943040 | tf_op jit(solution)/shard_map/contract/pallas_call | solution.py:102
  156.0 10.1 %collective-permute-start.27 = (f32[2,32,640]{2,1,0:T(8,128)S(1)}, f32[2,32,640]{2,1,0:T(8,128)S(1)}, u32[]{:S(2)}, u32[]{:S(2)}) collective-permute-start(f32[2,32,640]{2,1,0:T(8,128)S(1)} %copy-done.73), channel_id=1, source_target_pairs={{0,18},{2,16},{4,22},{6,20},{8,26},{10,24},{12,30},{14,28},{16,2},... | collective-permute-start | bytes 491528 | tf_op jit(solution)/shard_map/ppermute | solution.py:311
  170.7 9.8 %collective-permute-start.31 = (f32[2,32,640]{2,1,0:T(8,128)S(1)}, f32[2,32,640]{2,1,0:T(8,128)S(1)}, u32[]{:S(2)}, u32[]{:S(2)}) collective-permute-start(f32[2,32,640]{2,1,0:T(8,128)S(1)} %copy-done.68), channel_id=1, source_target_pairs={{0,26},{2,24},{4,30},{6,28},{8,18},{10,16},{12,22},{14,20},{16,10}... | collective-permute-start | bytes 491528 | tf_op jit(solution)/shard_map/ppermute | solution.py:311
  193.7 11.9 %combine.6 = (f32[2,128,640]{2,1,0:T(8,128)}, f32[2,128,640]{2,1,0:T(8,128)}, f32[2,128,640]{2,1,0:T(8,128)}, f32[2,128,640]{2,1,0:T(8,128)}, f32[2,128,640]{2,1...) custom-call(s32[1]{0:T(128)} %bitcast.4.me_ref, ...), custom_call_target="tpu_custom_call" | custom-call | flops 2621440 | bytes 31457280 | tf_op jit(solution)/shard_map/combine/pallas_call | solution.py:139
  205.7 17.1 %collective-permute-done.32.refs_14_ = f32[2,32,640]{2,1,0:T(8,128)S(1)} collective-permute-done((f32[2,32,640]{2,1,0:T(8,128)S(1)}, f32[2,32,640]{2,1,0:T(8,128)S(1)}, u32[]{:S(2)}, u32[]{:S(2)}) %collective-permute-start.32) | collective-permute-done | bytes 163872 | tf_op jit(solution)/shard_map/ppermute | solution.py:311
  231.1 18.5 %contract.7 = (f32[32,4,8,640]{3,2,1,0:T(8,128)}, f32[32,4,8,640]{3,2,1,0:T(8,128)}) custom-call(s32[25]{0:T(128)} %pad_add_fusion.info_ref, bf16[512,64]{1,0:T(8,128)(2,1)} %copy.13.occ_ref, bf16[640,8,4096]{2,1,0:T(8,128)(2,1)} %x_ref.7), custom_call_target="tpu_custom_call" | custom-call | flops 2684354560 | bytes 10485760 | tf_op jit(solution)/shard_map/contract/pallas_call | solution.py:102
  257.2 24.6 %collective-permute-done.41.refs_8_ = f32[2,64,640]{2,1,0:T(8,128)S(1)} collective-permute-done((f32[2,64,640]{2,1,0:T(8,128)}, f32[2,64,640]{2,1,0:T(8,128)S(1)}, u32[]{:S(2)}, u32[]{:S(2)}) %collective-permute-start.41) | collective-permute-done | bytes 327712 | tf_op jit(solution)/shard_map/ppermute | solution.py:311
  301.1 10.5 %collective-permute-done.46.refs_13_ = f32[2,64,640]{2,1,0:T(8,128)S(1)} collective-permute-done((f32[2,64,640]{2,1,0:T(8,128)}, f32[2,64,640]{2,1,0:T(8,128)S(1)}, u32[]{:S(2)}, u32[]{:S(2)}) %collective-permute-start.46) | collective-permute-done | bytes 327712 | tf_op jit(solution)/shard_map/ppermute | solution.py:311
  316.9 43.8 %collective-permute-done.47.refs_14_ = f32[2,64,640]{2,1,0:T(8,128)S(1)} collective-permute-done((f32[2,64,640]{2,1,0:T(8,128)}, f32[2,64,640]{2,1,0:T(8,128)S(1)}, u32[]{:S(2)}, u32[]{:S(2)}) %collective-permute-start.47) | collective-permute-done | bytes 327712 | tf_op jit(solution)/shard_map/ppermute | solution.py:311
  378.9 11.8 %collective-permute-done.52.refs_4_ = f32[2,128,640]{2,1,0:T(8,128)S(1)} collective-permute-done((f32[2,128,640]{2,1,0:T(8,128)}, f32[2,128,640]{2,1,0:T(8,128)S(1)}, u32[]{:S(2)}, u32[]{:S(2)}) %collective-permute-start.52) | collective-permute-done | bytes 655392 | tf_op jit(solution)/shard_map/ppermute | solution.py:311
  397.0 16.0 %collective-permute-start.57 = (f32[2,128,640]{2,1,0:T(8,128)}, f32[2,128,640]{2,1,0:T(8,128)S(1)}, u32[]{:S(2)}, u32[]{:S(2)}) collective-permute-start(f32[2,128,640]{2,1,0:T(8,128)} %get-tuple-element.178), channel_id=1, source_target_pairs={{0,18},{2,16},{4,22},{6,20},{8,26},{10,24},{12,30},{14,28},{16,2},... | collective-permute-start | bytes 1966088 | tf_op jit(solution)/shard_map/ppermute | solution.py:311
  429.8 36.0 %collective-permute-done.57.refs_9_ = f32[2,128,640]{2,1,0:T(8,128)S(1)} collective-permute-done((f32[2,128,640]{2,1,0:T(8,128)}, f32[2,128,640]{2,1,0:T(8,128)S(1)}, u32[]{:S(2)}, u32[]{:S(2)}) %collective-permute-start.57) | collective-permute-done | bytes 655392 | tf_op jit(solution)/shard_map/ppermute | solution.py:311
  470.5 10.1 %collective-permute-done.58.refs_10_ = f32[2,128,640]{2,1,0:T(8,128)S(1)} collective-permute-done((f32[2,128,640]{2,1,0:T(8,128)}, f32[2,128,640]{2,1,0:T(8,128)S(1)}, u32[]{:S(2)}, u32[]{:S(2)}) %collective-permute-start.58) | collective-permute-done | bytes 655392 | tf_op jit(solution)/shard_map/ppermute | solution.py:311
  491.3 36.6 %collective-permute-start.4 = (f32[2,32,640]{2,1,0:T(8,128)}, f32[2,32,640]{2,1,0:T(8,128)S(1)}, u32[]{:S(2)}, u32[]{:S(2)}) collective-permute-start(f32[2,32,640]{2,1,0:T(8,128)} %get-tuple-element.117), channel_id=1, source_target_pairs={{0,2},{2,0},{4,6},{6,4},{8,10},{10,8},{12,14},{14,12},{16,18},{18,... | collective-permute-start | bytes 491528 | tf_op jit(solution)/shard_map/ppermute | solution.py:311
  530.2 18.8 %collective-permute-done.62.refs_14_ = f32[2,128,640]{2,1,0:T(8,128)} collective-permute-done((f32[2,128,640]{2,1,0:T(8,128)}, f32[2,128,640]{2,1,0:T(8,128)}, u32[]{:S(2)}, u32[]{:S(2)}) %collective-permute-start.62) | collective-permute-done | bytes 655392 | tf_op jit(solution)/shard_map/ppermute | solution.py:311
  549.1 13.1 %collective-permute-start.8 = (f32[2,32,640]{2,1,0:T(8,128)}, f32[2,32,640]{2,1,0:T(8,128)S(1)}, u32[]{:S(2)}, u32[]{:S(2)}) collective-permute-start(f32[2,32,640]{2,1,0:T(8,128)} %get-tuple-element.121), channel_id=1, source_target_pairs={{0,10},{2,8},{4,14},{6,12},{8,2},{10,0},{12,6},{14,4},{16,26},{18,... | collective-permute-start | bytes 491528 | tf_op jit(solution)/shard_map/ppermute | solution.py:311
  562.2 14.6 %consume.4 = (bf16[2,128,2560]{2,1,0:T(8,128)(2,1)}, bf16[2,128,2560]{2,1,0:T(8,128)(2,1)}, f32[16,64,1024]{2,1,0:T(8,128)}) custom-call(s32[1]{0:T(128)} %bitcast.4.me_ref, f32[2,32,640]{2,1,0:T(8,128)} %get-tuple-element.132.refs_0_, f32[2,32,640]{2,1,0:T(8,128)} %copy-done.45, f32[2,32,640]{2,1,0:T(8,128)} %copy-done.46, f32[2,32,640]{2,1,0:T(8,128)} %copy-done.47, ...), custom_call_target="tpu_custom_call" | custom-call | flops 7214202880 | bytes 15728640 | tf_op jit(solution)/shard_map/consume/pallas_call | solution.py:253
  585.8 26.7 %consume.5 = (bf16[2,256,2560]{2,1,0:T(8,128)(2,1)}, bf16[2,256,2560]{2,1,0:T(8,128)(2,1)}, f32[16,64,1024]{2,1,0:T(8,128)}) custom-call(s32[1]{0:T(128)} %bitcast.4.me_ref, f32[2,64,640]{2,1,0:T(8,128)} %get-tuple-element.150.refs_0_, f32[2,64,640]{2,1,0:T(8,128)} %copy-done.27, f32[2,64,640]{2,1,0:T(8,128)} %copy-done.28, f32[2,64,640]{2,1,0:T(8,128)} %copy-done.29, ...), custom_call_target="tpu_custom_call" | custom-call | flops 16441671680 | bytes 18350080 | tf_op jit(solution)/shard_map/consume/pallas_call | solution.py:253
  624.8 60.7 %consume.6 = (bf16[2,512,2560]{2,1,0:T(8,128)(2,1)}, bf16[2,512,2560]{2,1,0:T(8,128)(2,1)}, f32[16,64,1024]{2,1,0:T(8,128)}) custom-call(s32[1]{0:T(128)} %bitcast.4.me_ref, f32[2,128,640]{2,1,0:T(8,128)} %get-tuple-element.169.refs_0_, f32[2,128,640]{2,1,0:T(8,128)} %copy-done.17, f32[2,128,640]{2,1,0:T(8,128)} %copy-done.18, f32[2,128,640]{2,1,0:T(8,128)} %copy-done.19, ...), custom_call_target="tpu_custom_call" | custom-call | flops 40936407040 | bytes 23592960 | tf_op jit(solution)/shard_map/consume/pallas_call | solution.py:253
  686.5 27.1 %consume.7 = f32[16,64,1024]{2,1,0:T(8,128)} custom-call(s32[1]{0:T(128)} %bitcast.4.me_ref, f32[2,32,640]{2,1,0:T(8,128)} %get-tuple-element.116.refs_0_, f32[2,32,640]{2,1,0:T(8,128)} %copy-done.2, f32[2,32,640]{2,1,0:T(8,128)} %copy-done.3, f32[2,32,640]{2,1,0:T(8,128)} %copy-done.4, f32[2,32,640]{2,1,0:T(8,128)} %copy-done.5, f32[2,32,640]{2,1,0:T(8,128)} %copy-done.6, ...), custom_call_target="tpu_custom_call" | custom-call | flops 10737418240 | bytes 15728640 | tf_op jit(solution)/shard_map/consume/pallas_call | solution.py:253
  713.7 48.5 %reduce-scatter.3.cloned.1.call-done = f32[2,64,1024]{2,1,0:T(8,128)} async-done(((f32[16,64,1024]{2,1,0:T(8,128)}), f32[2,64,1024]{2,1,0:T(8,128)}) %reduce-scatter.3.cloned.1.call-update) | async-done | bytes 524304 | tf_op jit(solution)/shard_map/reduce_scatter | solution.py:322
  764.4 22.0 %reduce-scatter.5.cloned.1.call-done = f32[256,128]{1,0:T(8,128)} async-done(((f32[1024,128]{1,0:T(8,128)}), f32[256,128]{1,0:T(8,128)}) %reduce-scatter.5.cloned.1.call-update) | async-done | bytes 131088 | tf_op jit(solution)/shard_map/reduce_scatter | solution.py:326
  (295 shorter events, 195.2 us)
Async XLA Ops:
  6.5 755.7 %reduce-scatter.3.cloned.1.call-start = ((), (), s32[]{:S(2)}) async-start(), calls=%async_computation.2 | async-start | bytes 4718592 | tf_op jit(solution)/shard_map/reduce_scatter | solution.py:322
  132.8 59.7 %collective-permute-start.2 = (f32[32,4,32,640]{3,2,1,0:T(8,128)}, f32[32,4,32,640]{3,2,1,0:T(8,128)}, u32[]{:S(2)}, u32[]{:S(2)}) collective-permute-start(f32[32,4,32,640]{3,2,1,0:T(8,128)} %get-tuple-element.108), channel_id=1, source_target_pairs={{0,1},{1,0},{2,3},{3,2},{4,5},{5,4},{6,7},{7,6},{8,9},{9,8},{10,11... | collective-permute-start | bytes 31457288 | tf_op jit(solution)/shard_map/ppermute | solution.py:304
  192.5 57.0 %collective-permute-start.36 = (f32[2,64,640]{2,1,0:T(8,128)S(1)}, f32[2,64,640]{2,1,0:T(8,128)S(1)}, u32[]{:S(2)}, u32[]{:S(2)}) collective-permute-start(f32[2,64,640]{2,1,0:T(8,128)S(1)} %copy-done.42), channel_id=1, source_target_pairs={{0,6},{2,4},{4,2},{6,0},{8,14},{10,12},{12,10},{14,8},{16,22},{18,... | collective-permute-start | bytes 983048 | tf_op jit(solution)/shard_map/ppermute | solution.py:311
  250.3 231.4 %collective-permute-start.3 = (f32[32,4,8,640]{3,2,1,0:T(8,128)}, f32[32,4,8,640]{3,2,1,0:T(8,128)S(1)}, u32[]{:S(2)}, u32[]{:S(2)}) collective-permute-start(f32[32,4,8,640]{3,2,1,0:T(8,128)} %get-tuple-element.113), channel_id=1, source_target_pairs={{0,1},{1,0},{2,3},{3,2},{4,5},{5,4},{6,7},{7,6},{8,9},{9,8},{10,11... | collective-permute-start | bytes 7864328 | tf_op jit(solution)/shard_map/ppermute | solution.py:304
  282.5 80.8 %collective-permute-start.49 = (f32[2,128,640]{2,1,0:T(8,128)}, f32[2,128,640]{2,1,0:T(8,128)S(1)}, u32[]{:S(2)}, u32[]{:S(2)}) collective-permute-start(f32[2,128,640]{2,1,0:T(8,128)} %get-tuple-element.170), channel_id=1, source_target_pairs={{0,2},{2,0},{4,6},{6,4},{8,10},{10,8},{12,14},{14,12},{16,18},{18,... | collective-permute-start | bytes 1966088 | tf_op jit(solution)/shard_map/ppermute | solution.py:311
  286.2 84.3 %collective-permute-start.50 = (f32[2,128,640]{2,1,0:T(8,128)}, f32[2,128,640]{2,1,0:T(8,128)S(1)}, u32[]{:S(2)}, u32[]{:S(2)}) collective-permute-start(f32[2,128,640]{2,1,0:T(8,128)} %get-tuple-element.171), channel_id=1, source_target_pairs={{0,4},{2,6},{4,0},{6,2},{8,12},{10,14},{12,8},{14,10},{16,20},{18,... | collective-permute-start | bytes 1966088 | tf_op jit(solution)/shard_map/ppermute | solution.py:311
  298.3 62.4 %collective-permute-start.47 = (f32[2,64,640]{2,1,0:T(8,128)}, f32[2,64,640]{2,1,0:T(8,128)S(1)}, u32[]{:S(2)}, u32[]{:S(2)}) collective-permute-start(f32[2,64,640]{2,1,0:T(8,128)} %get-tuple-element.164), channel_id=1, source_target_pairs={{0,28},{2,30},{4,24},{6,26},{8,20},{10,22},{12,16},{14,18},{16,12}... | collective-permute-start | bytes 983048 | tf_op jit(solution)/shard_map/ppermute | solution.py:311
  311.5 51.6 %collective-permute-start.48 = (f32[2,64,640]{2,1,0:T(8,128)}, f32[2,64,640]{2,1,0:T(8,128)S(1)}, u32[]{:S(2)}, u32[]{:S(2)}) collective-permute-start(f32[2,64,640]{2,1,0:T(8,128)} %get-tuple-element.165), channel_id=1, source_target_pairs={{0,30},{2,28},{4,26},{6,24},{8,22},{10,20},{12,18},{14,16},{16,14}... | collective-permute-start | bytes 983048 | tf_op jit(solution)/shard_map/ppermute | solution.py:311
  370.6 52.1 %collective-permute-start.54 = (f32[2,128,640]{2,1,0:T(8,128)}, f32[2,128,640]{2,1,0:T(8,128)S(1)}, u32[]{:S(2)}, u32[]{:S(2)}) collective-permute-start(f32[2,128,640]{2,1,0:T(8,128)} %get-tuple-element.175), channel_id=1, source_target_pairs={{0,12},{2,14},{4,8},{6,10},{8,4},{10,6},{12,0},{14,2},{16,28},{18,... | collective-permute-start | bytes 1966088 | tf_op jit(solution)/shard_map/ppermute | solution.py:311
  397.0 68.8 %collective-permute-start.57 = (f32[2,128,640]{2,1,0:T(8,128)}, f32[2,128,640]{2,1,0:T(8,128)S(1)}, u32[]{:S(2)}, u32[]{:S(2)}) collective-permute-start(f32[2,128,640]{2,1,0:T(8,128)} %get-tuple-element.178), channel_id=1, source_target_pairs={{0,18},{2,16},{4,22},{6,20},{8,26},{10,24},{12,30},{14,28},{16,2},... | collective-permute-start | bytes 1966088 | tf_op jit(solution)/shard_map/ppermute | solution.py:311
  422.7 58.0 %collective-permute-start.58 = (f32[2,128,640]{2,1,0:T(8,128)}, f32[2,128,640]{2,1,0:T(8,128)S(1)}, u32[]{:S(2)}, u32[]{:S(2)}) collective-permute-start(f32[2,128,640]{2,1,0:T(8,128)} %get-tuple-element.179), channel_id=1, source_target_pairs={{0,20},{2,22},{4,16},{6,18},{8,28},{10,30},{12,24},{14,26},{16,4},... | collective-permute-start | bytes 1966088 | tf_op jit(solution)/shard_map/ppermute | solution.py:311
  423.4 67.9 %collective-permute-start.59 = (f32[2,128,640]{2,1,0:T(8,128)}, f32[2,128,640]{2,1,0:T(8,128)}, u32[]{:S(2)}, u32[]{:S(2)}) collective-permute-start(f32[2,128,640]{2,1,0:T(8,128)} %get-tuple-element.180), channel_id=1, source_target_pairs={{0,22},{2,20},{4,18},{6,16},{8,30},{10,28},{12,26},{14,24},{16,6},... | collective-permute-start | bytes 1966088 | tf_op jit(solution)/shard_map/ppermute | solution.py:311
  429.2 98.6 %collective-permute-start.60 = (f32[2,128,640]{2,1,0:T(8,128)}, f32[2,128,640]{2,1,0:T(8,128)}, u32[]{:S(2)}, u32[]{:S(2)}) collective-permute-start(f32[2,128,640]{2,1,0:T(8,128)} %get-tuple-element.181), channel_id=1, source_target_pairs={{0,24},{2,26},{4,28},{6,30},{8,16},{10,18},{12,20},{14,22},{16,8},... | collective-permute-start | bytes 1966088 | tf_op jit(solution)/shard_map/ppermute | solution.py:311
  465.8 62.1 %collective-permute-start.61 = (f32[2,128,640]{2,1,0:T(8,128)}, f32[2,128,640]{2,1,0:T(8,128)}, u32[]{:S(2)}, u32[]{:S(2)}) collective-permute-start(f32[2,128,640]{2,1,0:T(8,128)} %get-tuple-element.182), channel_id=1, source_target_pairs={{0,26},{2,24},{4,30},{6,28},{8,18},{10,16},{12,22},{14,20},{16,10}... | collective-permute-start | bytes 1966088 | tf_op jit(solution)/shard_map/ppermute | solution.py:311
  480.6 68.5 %collective-permute-start.62 = (f32[2,128,640]{2,1,0:T(8,128)}, f32[2,128,640]{2,1,0:T(8,128)}, u32[]{:S(2)}, u32[]{:S(2)}) collective-permute-start(f32[2,128,640]{2,1,0:T(8,128)} %get-tuple-element.183), channel_id=1, source_target_pairs={{0,28},{2,30},{4,24},{6,26},{8,20},{10,22},{12,16},{14,18},{16,12}... | collective-permute-start | bytes 1966088 | tf_op jit(solution)/shard_map/ppermute | solution.py:311
  481.8 67.3 %collective-permute-start.63 = (f32[2,128,640]{2,1,0:T(8,128)}, f32[2,128,640]{2,1,0:T(8,128)}, u32[]{:S(2)}, u32[]{:S(2)}) collective-permute-start(f32[2,128,640]{2,1,0:T(8,128)} %get-tuple-element.184), channel_id=1, source_target_pairs={{0,30},{2,28},{4,26},{6,24},{8,22},{10,20},{12,18},{14,16},{16,14}... | collective-permute-start | bytes 1966088 | tf_op jit(solution)/shard_map/ppermute | solution.py:311
  491.3 85.6 %collective-permute-start.4 = (f32[2,32,640]{2,1,0:T(8,128)}, f32[2,32,640]{2,1,0:T(8,128)S(1)}, u32[]{:S(2)}, u32[]{:S(2)}) collective-permute-start(f32[2,32,640]{2,1,0:T(8,128)} %get-tuple-element.117), channel_id=1, source_target_pairs={{0,2},{2,0},{4,6},{6,4},{8,10},{10,8},{12,14},{14,12},{16,18},{18,... | collective-permute-start | bytes 491528 | tf_op jit(solution)/shard_map/ppermute | solution.py:311
  527.9 54.3 %collective-permute-start.6 = (f32[2,32,640]{2,1,0:T(8,128)}, f32[2,32,640]{2,1,0:T(8,128)S(1)}, u32[]{:S(2)}, u32[]{:S(2)}) collective-permute-start(f32[2,32,640]{2,1,0:T(8,128)} %get-tuple-element.119), channel_id=1, source_target_pairs={{0,6},{2,4},{4,2},{6,0},{8,14},{10,12},{12,10},{14,8},{16,22},{18,... | collective-permute-start | bytes 491528 | tf_op jit(solution)/shard_map/ppermute | solution.py:311
  612.6 73.0 %collective-permute-start.14 = (f32[2,32,640]{2,1,0:T(8,128)S(1)}, f32[2,32,640]{2,1,0:T(8,128)S(1)}, u32[]{:S(2)}, u32[]{:S(2)}) collective-permute-start(f32[2,32,640]{2,1,0:T(8,128)S(1)} %copy-done.65), channel_id=1, source_target_pairs={{0,22},{2,20},{4,18},{6,16},{8,30},{10,28},{12,26},{14,24},{16,6},... | collective-permute-start | bytes 491528 | tf_op jit(solution)/shard_map/ppermute | solution.py:311
  616.0 69.6 %collective-permute-start.15 = (f32[2,32,640]{2,1,0:T(8,128)S(1)}, f32[2,32,640]{2,1,0:T(8,128)S(1)}, u32[]{:S(2)}, u32[]{:S(2)}) collective-permute-start(f32[2,32,640]{2,1,0:T(8,128)S(1)} %copy-done.64), channel_id=1, source_target_pairs={{0,24},{2,26},{4,28},{6,30},{8,16},{10,18},{12,20},{14,22},{16,8},... | collective-permute-start | bytes 491528 | tf_op jit(solution)/shard_map/ppermute | solution.py:311
  616.5 69.1 %collective-permute-start.16 = (f32[2,32,640]{2,1,0:T(8,128)S(1)}, f32[2,32,640]{2,1,0:T(8,128)S(1)}, u32[]{:S(2)}, u32[]{:S(2)}) collective-permute-start(f32[2,32,640]{2,1,0:T(8,128)S(1)} %copy-done.63), channel_id=1, source_target_pairs={{0,26},{2,24},{4,30},{6,28},{8,18},{10,16},{12,22},{14,20},{16,10}... | collective-permute-start | bytes 491528 | tf_op jit(solution)/shard_map/ppermute | solution.py:311
  617.1 68.5 %collective-permute-start.17 = (f32[2,32,640]{2,1,0:T(8,128)S(1)}, f32[2,32,640]{2,1,0:T(8,128)S(1)}, u32[]{:S(2)}, u32[]{:S(2)}) collective-permute-start(f32[2,32,640]{2,1,0:T(8,128)S(1)} %copy-done.61), channel_id=1, source_target_pairs={{0,28},{2,30},{4,24},{6,26},{8,20},{10,22},{12,16},{14,18},{16,12}... | collective-permute-start | bytes 491528 | tf_op jit(solution)/shard_map/ppermute | solution.py:311
  620.5 65.1 %collective-permute-start.18 = (f32[2,32,640]{2,1,0:T(8,128)S(1)}, f32[2,32,640]{2,1,0:T(8,128)S(1)}, u32[]{:S(2)}, u32[]{:S(2)}) collective-permute-start(f32[2,32,640]{2,1,0:T(8,128)S(1)} %copy-done.60), channel_id=1, source_target_pairs={{0,30},{2,28},{4,26},{6,24},{8,22},{10,20},{12,18},{14,16},{16,14}... | collective-permute-start | bytes 491528 | tf_op jit(solution)/shard_map/ppermute | solution.py:311
  713.7 72.7 %reduce-scatter.5.cloned.1.call-start = ((), (), s32[]{:S(2)}) async-start(), calls=%async_computation.3 | async-start | bytes 655360 | tf_op jit(solution)/shard_map/reduce_scatter | solution.py:326
  (124 other events, 5134.4 us)
Sparse Core Ops, SparseCore 0:
  713.8 48.3 reduce-scatter.2
  764.5 21.8 reduce-scatter.4
where the time goes:
time: 794 us; the launch traced here: 793 us
  waiting for transfers between devices  295 us (37%)
  Pallas kernels  271 us (34%)
  starting transfers between devices  203 us (26%)
  between operations  14.2 us (2%)
    ppermute x60, waiting for transfers between devices, body(): lax.ppermute(pieces[d], ('aux', 'row'), pairs)  211 us
    ppermute x60, starting transfers between devices, body(): lax.ppermute(pieces[d], ('aux', 'row'), pairs)  201 us
    pallas_call x4, Pallas kernels, consume(): pl.pallas_call(functools.partial(consume_kernel, n_row=n_row, starts=star...  129 us
    pallas_call x4, Pallas kernels, contract(): pl.pallas_call(contract_kernel, grid_spec=pltpu.PrefetchScalarGridSpec(nu...  114 us
    reduce_scatter x1, waiting for transfers between devices, body(): lax.psum_scatter(total, ('aux', 'col'), scatter_dimension=0, tiled=True)  48.5 us
    pallas_call x4, Pallas kernels, combine(): pl.pallas_call(combine_kernel, in_specs=[pl.BlockSpec(memory_space=pltpu....  27.6 us
    reduce_scatter x1, waiting for transfers between devices, body(): return lax.psum_scatter(part, 'row', scatter_dimension=0, tiled=True)  22 us
  transfers between devices with their start and end apart: 66, of which 20 were waited for; matrix products, arithmetic and copies ran while one was open for 0% of the time, Pallas kernels for 17%

commit v1 on v0

--- a/solution.py
+++ b/solution.py
@@ -9,7 +9,7 @@
 
 BS = 64
 OCT = 8
-EIGHTHS = (1, 2, 4, 1)
+EIGHTHS = (2, 3, 2, 1)
 QT = 512
 VMEM_LIMIT = 60 * 1024 * 1024
 
@@ -267,6 +267,15 @@
     )(*args)
 
 
+def swap_sum(parts, axis, n):
+    me = lax.axis_index(axis)
+    own = lax.dynamic_index_in_dim(parts, me, 0, False)
+    for d in range(n - 1, 0, -1):
+        given = lax.dynamic_index_in_dim(parts, me ^ d, 0, False)
+        own = own + lax.ppermute(given, axis, [(s, s ^ d) for s in range(n)])
+    return own
+
+
 def body(integrals, pair_blocks, occupied, metric, nbf):
     n_aux, n_row, n_col = lax.axis_size("aux"), lax.axis_size("row"), lax.axis_size("col")
     occ = occupied.shape[1]
@@ -297,12 +306,21 @@
 
     sizes = tuple(e * BS // 8 for e in EIGHTHS)
     starts = tuple(sum(sizes[:c]) for c in range(len(sizes)))
-    arrived = []
-    for lo, m in zip(starts, sizes):
-        c = len(arrived)
-        other, mine = contract(info, occupied, integrals, lo, m, row_blocks)
+    count = len(sizes)
+    arrived, earlier, total = [], [], None
+
+    def use(c, me_array):
+        last = c == count - 1
+        return consume(me_array, arrived[c], metric, earlier, total, n_row, nbf, starts[: c + 1], sizes[: c + 1], last)
+
+    for c in range(count):
+        if c == count - 1:
+            *fitted, total = use(0, me_array)
+            earlier += fitted
+            info, total = lax.optimization_barrier((info, total))
+        other, mine = contract(info, occupied, integrals, starts[c], sizes[c], row_blocks)
         got = lax.ppermute(other, "col", [(0, 1), (1, 0)])
-        shape = (group, share, row_blocks * m, aux_rows)
+        shape = (group, share, row_blocks * sizes[c], aux_rows)
         pieces = list(combine(me_array, mine.reshape(shape), got.reshape(shape)))
         info, me_array, pieces[0] = lax.optimization_barrier((info, me_array, pieces[0]))
         sent = [None] * group
@@ -311,19 +329,20 @@
             sent[d] = pieces[d] if d == 0 else lax.ppermute(pieces[d], ("aux", "row"), pairs)
         arrived.append(sent)
 
-    earlier, total = [], None
-    for c in range(len(sizes)):
-        last = c == len(sizes) - 1
-        out = consume(me_array, arrived[c], metric, earlier, total, n_row, nbf, starts[: c + 1], sizes[: c + 1], last)
-        total = out[-1]
-        earlier += out[:-1]
-
+    for c in range(1, count):
+        *fitted, total = use(c, me_array)
+        earlier += fitted
+
+    halves = total.reshape(n_aux, n_col, -1, nbf)
+    col = lax.axis_index("col")
+    given = lax.dynamic_index_in_dim(halves, 1 - col, 1, False)
+    part = lax.dynamic_index_in_dim(halves, col, 1, False) + lax.ppermute(given, "col", [(0, 1), (1, 0)])
+    part = swap_sum(part, "aux", n_aux)
     blocks = nbf // BS
-    part = lax.psum_scatter(total, ("aux", "col"), scatter_dimension=0, tiled=True)
-    part = part.reshape(-1, nbf).T
+    part = part.T
     strips = [part[blocks * lo : blocks * (lo + m)].reshape(blocks, m, -1) for lo, m in zip(starts, sizes)]
-    part = jnp.concatenate(strips, 1).reshape(nbf, -1)
-    return lax.psum_scatter(part, "row", scatter_dimension=0, tiled=True)
+    part = jnp.concatenate(strips, 1).reshape(n_row, nbf // n_row, -1)
+    return swap_sum(part, "row", n_row)
 
 
 def solution(mesh):

time: 794 us -> 770 us (0.970)
  waiting for transfers between devices: 295 us -> 173 us
  starting transfers between devices: 203 us -> 312 us
  between operations: 14.2 us -> 0.79 us
    ppermute x60, starting transfers between devices: 201 us -> 303 us  [body(): lax.ppermute(pieces[d], ('aux', 'row'), pairs)]
    ppermute x60, waiting for transfers between devices: 211 us -> 117 us  [body(): lax.ppermute(pieces[d], ('aux', 'row'), pairs)]
    reduce_scatter x2 -> x0, waiting for transfers between devices: 70.5 us -> none  [the longest x1 48.5 us: body(): lax.psum_scatter(total, ('aux', 'col'), scatter_dimension=0, tiled=True)]
    ppermute x0 -> x7, waiting for transfers between devices: none -> 35 us  [the longest x6 30.7 us: swap_sum(): own = own + lax.ppermute(given, axis, [(s, s ^ d) for s in range(n)])]
    ppermute x0 -> x7, starting transfers between devices: none -> 8.01 us  [the longest x6 7.94 us: swap_sum(): own = own + lax.ppermute(given, axis, [(s, s ^ d) for s in range(n)])]
  transfers between devices with their start and end apart: 66 -> 71, of which waited for: 20 -> 26; matrix products, arithmetic and copies ran while one was open for 0% -> 0% of each run, Pallas kernels for 17% -> 17%
where the time goes in v1:
time: 770 us; the launch traced here: 769 us
  starting transfers between devices  312 us (41%)
  Pallas kernels  270 us (35%)
  waiting for transfers between devices  173 us (22%)
    ppermute x60, starting transfers between devices, body(): lax.ppermute(pieces[d], ('aux', 'row'), pairs)  303 us
    pallas_call x4, Pallas kernels, consume(): pl.pallas_call(functools.partial(consume_kernel, n_row=n_row, starts=star...  128 us
    ppermute x60, waiting for transfers between devices, body(): lax.ppermute(pieces[d], ('aux', 'row'), pairs)  117 us
    pallas_call x4, Pallas kernels, contract(): pl.pallas_call(contract_kernel, grid_spec=pltpu.PrefetchScalarGridSpec(nu...  114 us
    ppermute x6, waiting for transfers between devices, swap_sum(): own = own + lax.ppermute(given, axis, [(s, s ^ d) for s in range(n)])  30.7 us
    pallas_call x4, Pallas kernels, combine(): pl.pallas_call(combine_kernel, in_specs=[pl.BlockSpec(memory_space=pltpu....  27.5 us
    ppermute x4, waiting for transfers between devices, body(): got = lax.ppermute(other, 'col', [(0, 1), (1, 0)])  21 us
  transfers between devices with their start and end apart: 71, of which 26 were waited for; matrix products, arithmetic and copies ran while one was open for 0% of the time, Pallas kernels for 17%

profile of v1, /device:TPU:0, one launch (start us, length us, event | category | flops | bytes accessed | tf_op | source)
XLA Modules:
  0.0 769.3 jit_solution(18167130129388975916)
XLA Ops:
  3.6 28.6 %contract.4 = (f32[32,4,16,640]{3,2,1,0:T(8,128)}, f32[32,4,16,640]{3,2,1,0:T(8,128)}) custom-call(s32[25]{0:T(128)} %pad_add_fusion.info_ref, bf16[512,64]{1,0:T(8,128)(2,1)} %copy.18.occ_ref, bf16[640,8,4096]{2,1,0:T(8,128)(2,1)} %x_ref.7), custom_call_target="tpu_custom_call" | custom-call | flops 5368709120 | bytes 20971520 | tf_op jit(solution)/shard_map/contract/pallas_call | solution.py:102
  48.2 38.5 %contract.5 = (f32[32,4,24,640]{3,2,1,0:T(8,128)}, f32[32,4,24,640]{3,2,1,0:T(8,128)}) custom-call(s32[25]{0:T(128)} %pad_add_fusion.info_ref, bf16[512,64]{1,0:T(8,128)(2,1)} %copy.18.occ_ref, bf16[640,8,4096]{2,1,0:T(8,128)(2,1)} %x_ref.7), custom_call_target="tpu_custom_call" | custom-call | flops 8053063680 | bytes 31457280 | tf_op jit(solution)/shard_map/contract/pallas_call | solution.py:102
  87.1 12.4 %collective-permute-done.1 = f32[32,4,24,640]{3,2,1,0:T(8,128)} collective-permute-done((f32[32,4,24,640]{3,2,1,0:T(8,128)}, f32[32,4,24,640]{3,2,1,0:T(8,128)}, u32[]{:S(2)}, u32[]{:S(2)}) %collective-permute-start.1) | collective-permute-done | bytes 7864352 | tf_op jit(solution)/shard_map/ppermute | solution.py:322
  108.9 28.8 %contract.6 = (f32[32,4,16,640]{3,2,1,0:T(8,128)}, f32[32,4,16,640]{3,2,1,0:T(8,128)}) custom-call(s32[25]{0:T(128)} %pad_add_fusion.info_ref, bf16[512,64]{1,0:T(8,128)(2,1)} %copy.18.occ_ref, bf16[640,8,4096]{2,1,0:T(8,128)(2,1)} %x_ref.7), custom_call_target="tpu_custom_call" | custom-call | flops 5368709120 | bytes 20971520 | tf_op jit(solution)/shard_map/contract/pallas_call | solution.py:102
  173.9 18.4 %collective-permute-start.11 = (f32[2,64,640]{2,1,0:T(8,128)S(1)}, f32[2,64,640]{2,1,0:T(8,128)S(1)}, u32[]{:S(2)}, u32[]{:S(2)}) collective-permute-start(f32[2,64,640]{2,1,0:T(8,128)S(1)} %copy-done.53), channel_id=1, source_target_pairs={{0,18},{2,16},{4,22},{6,20},{8,26},{10,24},{12,30},{14,28},{16,2},... | collective-permute-start | bytes 983048 | tf_op jit(solution)/shard_map/ppermute | solution.py:329
  202.7 20.2 %collective-permute-start.15 = (f32[2,64,640]{2,1,0:T(8,128)S(1)}, f32[2,64,640]{2,1,0:T(8,128)}, u32[]{:S(2)}, u32[]{:S(2)}) collective-permute-start(f32[2,64,640]{2,1,0:T(8,128)S(1)} %copy-done.43), channel_id=1, source_target_pairs={{0,26},{2,24},{4,30},{6,28},{8,18},{10,16},{12,22},{14,20},{16,10}... | collective-permute-start | bytes 983048 | tf_op jit(solution)/shard_map/ppermute | solution.py:329
  235.0 13.8 %collective-permute-start.34 = (f32[2,96,640]{2,1,0:T(8,128)}, f32[2,96,640]{2,1,0:T(8,128)S(1)}, u32[]{:S(2)}, u32[]{:S(2)}) collective-permute-start(f32[2,96,640]{2,1,0:T(8,128)} %get-tuple-element.155), channel_id=1, source_target_pairs={{0,2},{2,0},{4,6},{6,4},{8,10},{10,8},{12,14},{14,12},{16,18},{18,... | collective-permute-start | bytes 1474568 | tf_op jit(solution)/shard_map/ppermute | solution.py:329
  256.7 23.3 %consume.4 = (bf16[2,256,2560]{2,1,0:T(8,128)(2,1)}, bf16[2,256,2560]{2,1,0:T(8,128)(2,1)}, f32[16,64,1024]{2,1,0:T(8,128)}) custom-call(s32[1]{0:T(128)} %bitcast.4.me_ref, f32[2,64,640]{2,1,0:T(8,128)} %get-tuple-element.114.refs_0_, f32[2,64,640]{2,1,0:T(8,128)} %copy-done.46, f32[2,64,640]{2,1,0:T(8,128)} %copy-done.47, f32[2,64,640]{2,1,0:T(8,128)} %copy-done.48, ...), custom_call_target="tpu_custom_call" | custom-call | flops 15435038720 | bytes 18350080 | tf_op jit(solution)/shard_map/consume/pallas_call | solution.py:253
  280.0 18.5 %contract.7 = (f32[32,4,8,640]{3,2,1,0:T(8,128)}, f32[32,4,8,640]{3,2,1,0:T(8,128)}) custom-call(s32[25]{0:T(128)} %pad_add_fusion.info_ref, bf16[512,64]{1,0:T(8,128)(2,1)} %copy.18.occ_ref, bf16[640,8,4096]{2,1,0:T(8,128)(2,1)} %x_ref.7), custom_call_target="tpu_custom_call" | custom-call | flops 2684354560 | bytes 10485760 | tf_op jit(solution)/shard_map/contract/pallas_call | solution.py:102
  299.7 29.0 %collective-permute-start.38 = (f32[2,96,640]{2,1,0:T(8,128)}, f32[2,96,640]{2,1,0:T(8,128)S(1)}, u32[]{:S(2)}, u32[]{:S(2)}) collective-permute-start(f32[2,96,640]{2,1,0:T(8,128)} %get-tuple-element.159), channel_id=1, source_target_pairs={{0,10},{2,8},{4,14},{6,12},{8,2},{10,0},{12,6},{14,4},{16,26},{18,... | collective-permute-start | bytes 1474568 | tf_op jit(solution)/shard_map/ppermute | solution.py:329
  332.2 17.1 %collective-permute-done.38.refs_5_ = f32[2,96,640]{2,1,0:T(8,128)S(1)} collective-permute-done((f32[2,96,640]{2,1,0:T(8,128)}, f32[2,96,640]{2,1,0:T(8,128)S(1)}, u32[]{:S(2)}, u32[]{:S(2)}) %collective-permute-start.38) | collective-permute-done | bytes 491552 | tf_op jit(solution)/shard_map/ppermute | solution.py:329
  349.2 14.3 %collective-permute-start.42 = (f32[2,96,640]{2,1,0:T(8,128)}, f32[2,96,640]{2,1,0:T(8,128)S(1)}, u32[]{:S(2)}, u32[]{:S(2)}) collective-permute-start(f32[2,96,640]{2,1,0:T(8,128)} %get-tuple-element.163), channel_id=1, source_target_pairs={{0,18},{2,16},{4,22},{6,20},{8,26},{10,24},{12,30},{14,28},{16,2},... | collective-permute-start | bytes 1474568 | tf_op jit(solution)/shard_map/ppermute | solution.py:329
  369.4 14.8 %collective-permute-done.42.refs_9_ = f32[2,96,640]{2,1,0:T(8,128)S(1)} collective-permute-done((f32[2,96,640]{2,1,0:T(8,128)}, f32[2,96,640]{2,1,0:T(8,128)S(1)}, u32[]{:S(2)}, u32[]{:S(2)}) %collective-permute-start.42) | collective-permute-done | bytes 491552 | tf_op jit(solution)/shard_map/ppermute | solution.py:329
  384.2 14.3 %collective-permute-start.46 = (f32[2,96,640]{2,1,0:T(8,128)}, f32[2,96,640]{2,1,0:T(8,128)S(1)}, u32[]{:S(2)}, u32[]{:S(2)}) collective-permute-start(f32[2,96,640]{2,1,0:T(8,128)} %get-tuple-element.167), channel_id=1, source_target_pairs={{0,26},{2,24},{4,30},{6,28},{8,18},{10,16},{12,22},{14,20},{16,10}... | collective-permute-start | bytes 1474568 | tf_op jit(solution)/shard_map/ppermute | solution.py:329
  410.8 33.1 %collective-permute-start.49 = (f32[2,64,640]{2,1,0:T(8,128)}, f32[2,64,640]{2,1,0:T(8,128)S(1)}, u32[]{:S(2)}, u32[]{:S(2)}) collective-permute-start(f32[2,64,640]{2,1,0:T(8,128)} %get-tuple-element.174), channel_id=1, source_target_pairs={{0,2},{2,0},{4,6},{6,4},{8,10},{10,8},{12,14},{14,12},{16,18},{18,... | collective-permute-start | bytes 983048 | tf_op jit(solution)/shard_map/ppermute | solution.py:329
  444.6 10.9 %collective-permute-done.47.refs_14_ = f32[2,96,640]{2,1,0:T(8,128)S(1)} collective-permute-done((f32[2,96,640]{2,1,0:T(8,128)}, f32[2,96,640]{2,1,0:T(8,128)S(1)}, u32[]{:S(2)}, u32[]{:S(2)}) %collective-permute-start.47) | collective-permute-done | bytes 491552 | tf_op jit(solution)/shard_map/ppermute | solution.py:329
  467.7 11.4 %collective-permute-start.53 = (f32[2,64,640]{2,1,0:T(8,128)}, f32[2,64,640]{2,1,0:T(8,128)S(1)}, u32[]{:S(2)}, u32[]{:S(2)}) collective-permute-start(f32[2,64,640]{2,1,0:T(8,128)} %get-tuple-element.178), channel_id=1, source_target_pairs={{0,10},{2,8},{4,14},{6,12},{8,2},{10,0},{12,6},{14,4},{16,26},{18,... | collective-permute-start | bytes 983048 | tf_op jit(solution)/shard_map/ppermute | solution.py:329
  489.8 17.9 %collective-permute-start.57 = (f32[2,64,640]{2,1,0:T(8,128)}, f32[2,64,640]{2,1,0:T(8,128)S(1)}, u32[]{:S(2)}, u32[]{:S(2)}) collective-permute-start(f32[2,64,640]{2,1,0:T(8,128)} %get-tuple-element.182), channel_id=1, source_target_pairs={{0,18},{2,16},{4,22},{6,20},{8,26},{10,24},{12,30},{14,28},{16,2},... | collective-permute-start | bytes 983048 | tf_op jit(solution)/shard_map/ppermute | solution.py:329
  519.9 18.3 %collective-permute-start.61 = (f32[2,64,640]{2,1,0:T(8,128)}, f32[2,64,640]{2,1,0:T(8,128)}, u32[]{:S(2)}, u32[]{:S(2)}) collective-permute-start(f32[2,64,640]{2,1,0:T(8,128)} %get-tuple-element.186), channel_id=1, source_target_pairs={{0,26},{2,24},{4,30},{6,28},{8,18},{10,16},{12,22},{14,20},{16,10}... | collective-permute-start | bytes 983048 | tf_op jit(solution)/shard_map/ppermute | solution.py:329
  548.7 21.0 %collective-permute-start.19 = (f32[2,32,640]{2,1,0:T(8,128)}, f32[2,32,640]{2,1,0:T(8,128)S(1)}, u32[]{:S(2)}, u32[]{:S(2)}) collective-permute-start(f32[2,32,640]{2,1,0:T(8,128)} %get-tuple-element.137), channel_id=1, source_target_pairs={{0,2},{2,0},{4,6},{6,4},{8,10},{10,8},{12,14},{14,12},{16,18},{18,... | collective-permute-start | bytes 491528 | tf_op jit(solution)/shard_map/ppermute | solution.py:329
  601.2 44.2 %consume.5 = (bf16[2,384,2560]{2,1,0:T(8,128)(2,1)}, bf16[2,384,2560]{2,1,0:T(8,128)(2,1)}, f32[16,64,1024]{2,1,0:T(8,128)}) custom-call(s32[1]{0:T(128)} %bitcast.4.me_ref, f32[2,96,640]{2,1,0:T(8,128)} %get-tuple-element.154.refs_0_, f32[2,96,640]{2,1,0:T(8,128)} %copy-done.16, f32[2,96,640]{2,1,0:T(8,128)} %copy-done.17, f32[2,96,640]{2,1,0:T(8,128)} %copy-done.18, ...), custom_call_target="tpu_custom_call" | custom-call | flops 27682406400 | bytes 20971520 | tf_op jit(solution)/shard_map/consume/pallas_call | solution.py:253
  657.0 31.9 %consume.6 = (bf16[2,256,2560]{2,1,0:T(8,128)(2,1)}, bf16[2,256,2560]{2,1,0:T(8,128)(2,1)}, f32[16,64,1024]{2,1,0:T(8,128)}) custom-call(s32[1]{0:T(128)} %bitcast.4.me_ref, f32[2,64,640]{2,1,0:T(8,128)} %get-tuple-element.173.refs_0_, f32[2,64,640]{2,1,0:T(8,128)} %copy-done.31, f32[2,64,640]{2,1,0:T(8,128)} %copy-done.32, f32[2,64,640]{2,1,0:T(8,128)} %copy-done.33, ...), custom_call_target="tpu_custom_call" | custom-call | flops 20468203520 | bytes 18350080 | tf_op jit(solution)/shard_map/consume/pallas_call | solution.py:253
  689.9 28.3 %consume.7 = f32[16,64,1024]{2,1,0:T(8,128)} custom-call(s32[1]{0:T(128)} %bitcast.4.me_ref, f32[2,32,640]{2,1,0:T(8,128)} %get-tuple-element.136.refs_0_, f32[2,32,640]{2,1,0:T(8,128)} %copy-done.1, f32[2,32,640]{2,1,0:T(8,128)} %copy-done.2, f32[2,32,640]{2,1,0:T(8,128)} %copy-done.3, f32[2,32,640]{2,1,0:T(8,128)} %copy-done.4, f32[2,32,640]{2,1,0:T(8,128)} %copy-done.5, ...), custom_call_target="tpu_custom_call" | custom-call | flops 10737418240 | bytes 15728640 | tf_op jit(solution)/shard_map/consume/pallas_call | solution.py:253
  731.4 11.6 %collective-permute-done.67 = f32[128,1024]{1,0:T(8,128)} collective-permute-done((f32[128,1024]{1,0:T(8,128)}, f32[128,1024]{1,0:T(8,128)}, u32[]{:S(2)}, u32[]{:S(2)}) %collective-permute-start.67) | collective-permute-done | bytes 524320 | tf_op jit(solution)/shard_map/ppermute | solution.py:275
  (282 shorter events, 248.0 us)
Async XLA Ops:
  137.7 87.3 %collective-permute-start.2 = (f32[32,4,16,640]{3,2,1,0:T(8,128)}, f32[32,4,16,640]{3,2,1,0:T(8,128)}, u32[]{:S(2)}, u32[]{:S(2)}) collective-permute-start(f32[32,4,16,640]{3,2,1,0:T(8,128)} %get-tuple-element.110), channel_id=1, source_target_pairs={{0,1},{1,0},{2,3},{3,2},{4,5},{5,4},{6,7},{7,6},{8,9},{9,8},{10,11... | collective-permute-start | bytes 15728648 | tf_op jit(solution)/shard_map/ppermute | solution.py:322
  199.2 49.6 %collective-permute-start.14 = (f32[2,64,640]{2,1,0:T(8,128)S(1)}, f32[2,64,640]{2,1,0:T(8,128)S(1)}, u32[]{:S(2)}, u32[]{:S(2)}) collective-permute-start(f32[2,64,640]{2,1,0:T(8,128)S(1)} %copy-done.44), channel_id=1, source_target_pairs={{0,24},{2,26},{4,28},{6,30},{8,16},{10,18},{12,20},{14,22},{16,8},... | collective-permute-start | bytes 983048 | tf_op jit(solution)/shard_map/ppermute | solution.py:329
  202.7 47.5 %collective-permute-start.15 = (f32[2,64,640]{2,1,0:T(8,128)S(1)}, f32[2,64,640]{2,1,0:T(8,128)}, u32[]{:S(2)}, u32[]{:S(2)}) collective-permute-start(f32[2,64,640]{2,1,0:T(8,128)S(1)} %copy-done.43), channel_id=1, source_target_pairs={{0,26},{2,24},{4,30},{6,28},{8,18},{10,16},{12,22},{14,20},{16,10}... | collective-permute-start | bytes 983048 | tf_op jit(solution)/shard_map/ppermute | solution.py:329
  235.0 64.7 %collective-permute-start.34 = (f32[2,96,640]{2,1,0:T(8,128)}, f32[2,96,640]{2,1,0:T(8,128)S(1)}, u32[]{:S(2)}, u32[]{:S(2)}) collective-permute-start(f32[2,96,640]{2,1,0:T(8,128)} %get-tuple-element.155), channel_id=1, source_target_pairs={{0,2},{2,0},{4,6},{6,4},{8,10},{10,8},{12,14},{14,12},{16,18},{18,... | collective-permute-start | bytes 1474568 | tf_op jit(solution)/shard_map/ppermute | solution.py:329
  249.5 79.2 %collective-permute-start.35 = (f32[2,96,640]{2,1,0:T(8,128)}, f32[2,96,640]{2,1,0:T(8,128)S(1)}, u32[]{:S(2)}, u32[]{:S(2)}) collective-permute-start(f32[2,96,640]{2,1,0:T(8,128)} %get-tuple-element.156), channel_id=1, source_target_pairs={{0,4},{2,6},{4,0},{6,2},{8,12},{10,14},{12,8},{14,10},{16,20},{18,... | collective-permute-start | bytes 1474568 | tf_op jit(solution)/shard_map/ppermute | solution.py:329
  250.2 78.9 %collective-permute-start.36 = (f32[2,96,640]{2,1,0:T(8,128)}, f32[2,96,640]{2,1,0:T(8,128)S(1)}, u32[]{:S(2)}, u32[]{:S(2)}) collective-permute-start(f32[2,96,640]{2,1,0:T(8,128)} %get-tuple-element.157), channel_id=1, source_target_pairs={{0,6},{2,4},{4,2},{6,0},{8,14},{10,12},{12,10},{14,8},{16,22},{18,... | collective-permute-start | bytes 1474568 | tf_op jit(solution)/shard_map/ppermute | solution.py:329
  298.5 242.7 %collective-permute-start.18 = (f32[32,4,8,640]{3,2,1,0:T(8,128)}, f32[32,4,8,640]{3,2,1,0:T(8,128)S(1)}, u32[]{:S(2)}, u32[]{:S(2)}) collective-permute-start(f32[32,4,8,640]{3,2,1,0:T(8,128)} %get-tuple-element.133), channel_id=1, source_target_pairs={{0,1},{1,0},{2,3},{3,2},{4,5},{5,4},{6,7},{7,6},{8,9},{9,8},{10,11... | collective-permute-start | bytes 7864328 | tf_op jit(solution)/shard_map/ppermute | solution.py:322
  299.7 49.5 %collective-permute-start.38 = (f32[2,96,640]{2,1,0:T(8,128)}, f32[2,96,640]{2,1,0:T(8,128)S(1)}, u32[]{:S(2)}, u32[]{:S(2)}) collective-permute-start(f32[2,96,640]{2,1,0:T(8,128)} %get-tuple-element.159), channel_id=1, source_target_pairs={{0,10},{2,8},{4,14},{6,12},{8,2},{10,0},{12,6},{14,4},{16,26},{18,... | collective-permute-start | bytes 1474568 | tf_op jit(solution)/shard_map/ppermute | solution.py:329
  365.8 42.0 %collective-permute-start.43 = (f32[2,96,640]{2,1,0:T(8,128)}, f32[2,96,640]{2,1,0:T(8,128)S(1)}, u32[]{:S(2)}, u32[]{:S(2)}) collective-permute-start(f32[2,96,640]{2,1,0:T(8,128)} %get-tuple-element.164), channel_id=1, source_target_pairs={{0,20},{2,22},{4,16},{6,18},{8,28},{10,30},{12,24},{14,26},{16,4},... | collective-permute-start | bytes 1474568 | tf_op jit(solution)/shard_map/ppermute | solution.py:329
  365.8 42.1 %collective-permute-start.44 = (f32[2,96,640]{2,1,0:T(8,128)}, f32[2,96,640]{2,1,0:T(8,128)S(1)}, u32[]{:S(2)}, u32[]{:S(2)}) collective-permute-start(f32[2,96,640]{2,1,0:T(8,128)} %get-tuple-element.165), channel_id=1, source_target_pairs={{0,22},{2,20},{4,18},{6,16},{8,30},{10,28},{12,26},{14,24},{16,6},... | collective-permute-start | bytes 1474568 | tf_op jit(solution)/shard_map/ppermute | solution.py:329
  368.3 42.4 %collective-permute-start.45 = (f32[2,96,640]{2,1,0:T(8,128)}, f32[2,96,640]{2,1,0:T(8,128)S(1)}, u32[]{:S(2)}, u32[]{:S(2)}) collective-permute-start(f32[2,96,640]{2,1,0:T(8,128)} %get-tuple-element.166), channel_id=1, source_target_pairs={{0,24},{2,26},{4,28},{6,30},{8,16},{10,18},{12,20},{14,22},{16,8},... | collective-permute-start | bytes 1474568 | tf_op jit(solution)/shard_map/ppermute | solution.py:329
  384.2 59.6 %collective-permute-start.46 = (f32[2,96,640]{2,1,0:T(8,128)}, f32[2,96,640]{2,1,0:T(8,128)S(1)}, u32[]{:S(2)}, u32[]{:S(2)}) collective-permute-start(f32[2,96,640]{2,1,0:T(8,128)} %get-tuple-element.167), channel_id=1, source_target_pairs={{0,26},{2,24},{4,30},{6,28},{8,18},{10,16},{12,22},{14,20},{16,10}... | collective-permute-start | bytes 1474568 | tf_op jit(solution)/shard_map/ppermute | solution.py:329
  407.8 47.8 %collective-permute-start.47 = (f32[2,96,640]{2,1,0:T(8,128)}, f32[2,96,640]{2,1,0:T(8,128)S(1)}, u32[]{:S(2)}, u32[]{:S(2)}) collective-permute-start(f32[2,96,640]{2,1,0:T(8,128)} %get-tuple-element.168), channel_id=1, source_target_pairs={{0,28},{2,30},{4,24},{6,26},{8,20},{10,22},{12,16},{14,18},{16,12}... | collective-permute-start | bytes 1474568 | tf_op jit(solution)/shard_map/ppermute | solution.py:329
  407.9 49.4 %collective-permute-start.48 = (f32[2,96,640]{2,1,0:T(8,128)}, f32[2,96,640]{2,1,0:T(8,128)S(1)}, u32[]{:S(2)}, u32[]{:S(2)}) collective-permute-start(f32[2,96,640]{2,1,0:T(8,128)} %get-tuple-element.169), channel_id=1, source_target_pairs={{0,30},{2,28},{4,26},{6,24},{8,22},{10,20},{12,18},{14,16},{16,14}... | collective-permute-start | bytes 1474568 | tf_op jit(solution)/shard_map/ppermute | solution.py:329
  410.8 57.0 %collective-permute-start.49 = (f32[2,64,640]{2,1,0:T(8,128)}, f32[2,64,640]{2,1,0:T(8,128)S(1)}, u32[]{:S(2)}, u32[]{:S(2)}) collective-permute-start(f32[2,64,640]{2,1,0:T(8,128)} %get-tuple-element.174), channel_id=1, source_target_pairs={{0,2},{2,0},{4,6},{6,4},{8,10},{10,8},{12,14},{14,12},{16,18},{18,... | collective-permute-start | bytes 983048 | tf_op jit(solution)/shard_map/ppermute | solution.py:329
  514.4 55.4 %collective-permute-start.60 = (f32[2,64,640]{2,1,0:T(8,128)}, f32[2,64,640]{2,1,0:T(8,128)}, u32[]{:S(2)}, u32[]{:S(2)}) collective-permute-start(f32[2,64,640]{2,1,0:T(8,128)} %get-tuple-element.185), channel_id=1, source_target_pairs={{0,24},{2,26},{4,28},{6,30},{8,16},{10,18},{12,20},{14,22},{16,8},... | collective-permute-start | bytes 983048 | tf_op jit(solution)/shard_map/ppermute | solution.py:329
  519.9 49.8 %collective-permute-start.61 = (f32[2,64,640]{2,1,0:T(8,128)}, f32[2,64,640]{2,1,0:T(8,128)}, u32[]{:S(2)}, u32[]{:S(2)}) collective-permute-start(f32[2,64,640]{2,1,0:T(8,128)} %get-tuple-element.186), channel_id=1, source_target_pairs={{0,26},{2,24},{4,30},{6,28},{8,18},{10,16},{12,22},{14,20},{16,10}... | collective-permute-start | bytes 983048 | tf_op jit(solution)/shard_map/ppermute | solution.py:329
  588.2 57.3 %collective-permute-start.24 = (f32[2,32,640]{2,1,0:T(8,128)}, f32[2,32,640]{2,1,0:T(8,128)S(1)}, u32[]{:S(2)}, u32[]{:S(2)}) collective-permute-start(f32[2,32,640]{2,1,0:T(8,128)} %get-tuple-element.142), channel_id=1, source_target_pairs={{0,12},{2,14},{4,8},{6,10},{8,4},{10,6},{12,0},{14,2},{16,28},{18,... | collective-permute-start | bytes 491528 | tf_op jit(solution)/shard_map/ppermute | solution.py:329
  590.0 58.2 %collective-permute-start.25 = (f32[2,32,640]{2,1,0:T(8,128)}, f32[2,32,640]{2,1,0:T(8,128)S(1)}, u32[]{:S(2)}, u32[]{:S(2)}) collective-permute-start(f32[2,32,640]{2,1,0:T(8,128)} %get-tuple-element.143), channel_id=1, source_target_pairs={{0,14},{2,12},{4,10},{6,8},{8,6},{10,4},{12,2},{14,0},{16,30},{18,... | collective-permute-start | bytes 491528 | tf_op jit(solution)/shard_map/ppermute | solution.py:329
  591.8 57.3 %collective-permute-start.26 = (f32[2,32,640]{2,1,0:T(8,128)}, f32[2,32,640]{2,1,0:T(8,128)S(1)}, u32[]{:S(2)}, u32[]{:S(2)}) collective-permute-start(f32[2,32,640]{2,1,0:T(8,128)} %get-tuple-element.144), channel_id=1, source_target_pairs={{0,16},{2,18},{4,20},{6,22},{8,24},{10,26},{12,28},{14,30},{16,0},... | collective-permute-start | bytes 491528 | tf_op jit(solution)/shard_map/ppermute | solution.py:329
  593.2 58.6 %collective-permute-start.27 = (f32[2,32,640]{2,1,0:T(8,128)}, f32[2,32,640]{2,1,0:T(8,128)S(1)}, u32[]{:S(2)}, u32[]{:S(2)}) collective-permute-start(f32[2,32,640]{2,1,0:T(8,128)} %get-tuple-element.145), channel_id=1, source_target_pairs={{0,18},{2,16},{4,22},{6,20},{8,26},{10,24},{12,30},{14,28},{16,2},... | collective-permute-start | bytes 491528 | tf_op jit(solution)/shard_map/ppermute | solution.py:329
  600.5 53.5 %collective-permute-start.28 = (f32[2,32,640]{2,1,0:T(8,128)}, f32[2,32,640]{2,1,0:T(8,128)S(1)}, u32[]{:S(2)}, u32[]{:S(2)}) collective-permute-start(f32[2,32,640]{2,1,0:T(8,128)} %get-tuple-element.146), channel_id=1, source_target_pairs={{0,20},{2,22},{4,16},{6,18},{8,28},{10,30},{12,24},{14,26},{16,4},... | collective-permute-start | bytes 491528 | tf_op jit(solution)/shard_map/ppermute | solution.py:329
  645.5 43.5 %collective-permute-start.29 = (f32[2,32,640]{2,1,0:T(8,128)S(1)}, f32[2,32,640]{2,1,0:T(8,128)S(1)}, u32[]{:S(2)}, u32[]{:S(2)}) collective-permute-start(f32[2,32,640]{2,1,0:T(8,128)S(1)} %copy-done.66), channel_id=1, source_target_pairs={{0,22},{2,20},{4,18},{6,16},{8,30},{10,28},{12,26},{14,24},{16,6},... | collective-permute-start | bytes 491528 | tf_op jit(solution)/shard_map/ppermute | solution.py:329
  648.2 40.8 %collective-permute-start.30 = (f32[2,32,640]{2,1,0:T(8,128)S(1)}, f32[2,32,640]{2,1,0:T(8,128)S(1)}, u32[]{:S(2)}, u32[]{:S(2)}) collective-permute-start(f32[2,32,640]{2,1,0:T(8,128)S(1)} %copy-done.65), channel_id=1, source_target_pairs={{0,24},{2,26},{4,28},{6,30},{8,16},{10,18},{12,20},{14,22},{16,8},... | collective-permute-start | bytes 491528 | tf_op jit(solution)/shard_map/ppermute | solution.py:329
  (114 other events, 6256.9 us)

commit v2 on v1

--- a/solution.py
+++ b/solution.py
@@ -9,7 +9,7 @@
 
 BS = 64
 OCT = 8
-EIGHTHS = (2, 3, 2, 1)
+EIGHTHS = (2, 2, 3, 1)
 QT = 512
 VMEM_LIMIT = 60 * 1024 * 1024
 
@@ -315,8 +315,9 @@
 
     for c in range(count):
         if c == count - 1:
-            *fitted, total = use(0, me_array)
-            earlier += fitted
+            for early in range(count - 2):
+                *fitted, total = use(early, me_array)
+                earlier += fitted
             info, total = lax.optimization_barrier((info, total))
         other, mine = contract(info, occupied, integrals, starts[c], sizes[c], row_blocks)
         got = lax.ppermute(other, "col", [(0, 1), (1, 0)])
@@ -329,7 +330,7 @@
             sent[d] = pieces[d] if d == 0 else lax.ppermute(pieces[d], ("aux", "row"), pairs)
         arrived.append(sent)
 
-    for c in range(1, count):
+    for c in range(count - 2, count):
         *fitted, total = use(c, me_array)
         earlier += fitted
 

time: 770 us -> 770 us (level)
  waiting for transfers between devices: 173 us -> 215 us
  starting transfers between devices: 312 us -> 275 us
    ppermute x60, waiting for transfers between devices: 117 us -> 162 us  [body(): lax.ppermute(pieces[d], ('aux', 'row'), pairs)]
    ppermute x60, starting transfers between devices: 303 us -> 266 us  [body(): lax.ppermute(pieces[d], ('aux', 'row'), pairs)]
  transfers between devices with their start and end apart: 71 -> 71, of which waited for: 26 -> 28; matrix products, arithmetic and copies ran while one was open for 0% -> 0% of each run, Pallas kernels for 17% -> 10%
where the time goes in v2:
time: 770 us
  starting transfers between devices  275 us (36%)
  Pallas kernels  265 us (34%)
  waiting for transfers between devices  215 us (28%)
    ppermute x60, starting transfers between devices, body(): lax.ppermute(pieces[d], ('aux', 'row'), pairs)  266 us
    ppermute x60, waiting for transfers between devices, body(): lax.ppermute(pieces[d], ('aux', 'row'), pairs)  162 us
    pallas_call x4, Pallas kernels, consume(): pl.pallas_call(functools.partial(consume_kernel, n_row=n_row, starts=star...  122 us
    pallas_call x4, Pallas kernels, contract(): pl.pallas_call(contract_kernel, grid_spec=pltpu.PrefetchScalarGridSpec(nu...  114 us
    ppermute x6, waiting for transfers between devices, swap_sum(): own = own + lax.ppermute(given, axis, [(s, s ^ d) for s in range(n)])  31.2 us
    pallas_call x4, Pallas kernels, combine(): pl.pallas_call(combine_kernel, in_specs=[pl.BlockSpec(memory_space=pltpu....  27.6 us
    ppermute x4, waiting for transfers between devices, body(): got = lax.ppermute(other, 'col', [(0, 1), (1, 0)])  17.3 us
  transfers between devices with their start and end apart: 71, of which 28 were waited for; matrix products, arithmetic and copies ran while one was open for 0% of the time, Pallas kernels for 10%

profile of v2, /device:TPU:0, one launch (start us, length us, event | category | flops | bytes accessed | tf_op | source)
XLA Modules:
  0.0 769.6 jit_solution(2527206871741399122)
XLA Ops:
  3.7 28.6 %contract.4 = (f32[32,4,16,640]{3,2,1,0:T(8,128)}, f32[32,4,16,640]{3,2,1,0:T(8,128)}) custom-call(s32[25]{0:T(128)} %pad_add_fusion.info_ref, bf16[512,64]{1,0:T(8,128)(2,1)} %copy.18.occ_ref, bf16[640,8,4096]{2,1,0:T(8,128)(2,1)} %x_ref.7), custom_call_target="tpu_custom_call" | custom-call | flops 5368709120 | bytes 20971520 | tf_op jit(solution)/shard_map/contract/pallas_call | solution.py:102
  48.4 28.6 %contract.5 = (f32[32,4,16,640]{3,2,1,0:T(8,128)}, f32[32,4,16,640]{3,2,1,0:T(8,128)}) custom-call(s32[25]{0:T(128)} %pad_add_fusion.info_ref, bf16[512,64]{1,0:T(8,128)(2,1)} %copy.18.occ_ref, bf16[640,8,4096]{2,1,0:T(8,128)(2,1)} %x_ref.7), custom_call_target="tpu_custom_call" | custom-call | flops 5368709120 | bytes 20971520 | tf_op jit(solution)/shard_map/contract/pallas_call | solution.py:102
  92.9 38.6 %contract.6 = (f32[32,4,24,640]{3,2,1,0:T(8,128)}, f32[32,4,24,640]{3,2,1,0:T(8,128)}) custom-call(s32[25]{0:T(128)} %pad_add_fusion.info_ref, bf16[512,64]{1,0:T(8,128)(2,1)} %copy.18.occ_ref, bf16[640,8,4096]{2,1,0:T(8,128)(2,1)} %x_ref.7), custom_call_target="tpu_custom_call" | custom-call | flops 8053063680 | bytes 31457280 | tf_op jit(solution)/shard_map/contract/pallas_call | solution.py:102
  138.9 10.7 %collective-permute-done.18.refs_1_ = f32[2,64,640]{2,1,0:T(8,128)S(1)} collective-permute-done((f32[2,64,640]{2,1,0:T(8,128)}, f32[2,64,640]{2,1,0:T(8,128)S(1)}, u32[]{:S(2)}, u32[]{:S(2)}) %collective-permute-start.18) | collective-permute-done | bytes 327712 | tf_op jit(solution)/shard_map/ppermute | solution.py:330
  167.8 18.4 %collective-permute-start.26 = (f32[2,64,640]{2,1,0:T(8,128)}, f32[2,64,640]{2,1,0:T(8,128)S(1)}, u32[]{:S(2)}, u32[]{:S(2)}) collective-permute-start(f32[2,64,640]{2,1,0:T(8,128)} %get-tuple-element.139), channel_id=1, source_target_pairs={{0,18},{2,16},{4,22},{6,20},{8,26},{10,24},{12,30},{14,28},{16,2},... | collective-permute-start | bytes 983048 | tf_op jit(solution)/shard_map/ppermute | solution.py:330
  196.6 20.2 %collective-permute-start.30 = (f32[2,64,640]{2,1,0:T(8,128)}, f32[2,64,640]{2,1,0:T(8,128)S(1)}, u32[]{:S(2)}, u32[]{:S(2)}) collective-permute-start(f32[2,64,640]{2,1,0:T(8,128)} %get-tuple-element.143), channel_id=1, source_target_pairs={{0,26},{2,24},{4,30},{6,28},{8,18},{10,16},{12,22},{14,20},{16,10}... | collective-permute-start | bytes 983048 | tf_op jit(solution)/shard_map/ppermute | solution.py:330
  221.9 23.8 %collective-permute-start.3 = (f32[2,64,640]{2,1,0:T(8,128)}, f32[2,64,640]{2,1,0:T(8,128)S(1)}, u32[]{:S(2)}, u32[]{:S(2)}) collective-permute-start(f32[2,64,640]{2,1,0:T(8,128)} %get-tuple-element.115), channel_id=1, source_target_pairs={{0,2},{2,0},{4,6},{6,4},{8,10},{10,8},{12,14},{14,12},{16,18},{18,... | collective-permute-start | bytes 983048 | tf_op jit(solution)/shard_map/ppermute | solution.py:330
  256.3 17.4 %collective-permute-start.7 = (f32[2,64,640]{2,1,0:T(8,128)S(1)}, f32[2,64,640]{2,1,0:T(8,128)S(1)}, u32[]{:S(2)}, u32[]{:S(2)}) collective-permute-start(f32[2,64,640]{2,1,0:T(8,128)S(1)} %copy-done.47), channel_id=1, source_target_pairs={{0,10},{2,8},{4,14},{6,12},{8,2},{10,0},{12,6},{14,4},{16,26},{18,... | collective-permute-start | bytes 983048 | tf_op jit(solution)/shard_map/ppermute | solution.py:330
  284.1 18.4 %collective-permute-start.11 = (f32[2,64,640]{2,1,0:T(8,128)S(1)}, f32[2,64,640]{2,1,0:T(8,128)}, u32[]{:S(2)}, u32[]{:S(2)}) collective-permute-start(f32[2,64,640]{2,1,0:T(8,128)S(1)} %copy-done.36), channel_id=1, source_target_pairs={{0,18},{2,16},{4,22},{6,20},{8,26},{10,24},{12,30},{14,28},{16,2},... | collective-permute-start | bytes 983048 | tf_op jit(solution)/shard_map/ppermute | solution.py:330
  316.1 16.6 %collective-permute-start.15 = (f32[2,64,640]{2,1,0:T(8,128)S(1)}, f32[2,64,640]{2,1,0:T(8,128)S(1)}, u32[]{:S(2)}, u32[]{:S(2)}) collective-permute-start(f32[2,64,640]{2,1,0:T(8,128)S(1)} %copy-done.31), channel_id=1, source_target_pairs={{0,26},{2,24},{4,30},{6,28},{8,18},{10,16},{12,22},{14,20},{16,10}... | collective-permute-start | bytes 983048 | tf_op jit(solution)/shard_map/ppermute | solution.py:330
  332.6 12.8 %collective-permute-done.12.refs_10_ = f32[2,64,640]{2,1,0:T(8,128)} collective-permute-done((f32[2,64,640]{2,1,0:T(8,128)S(1)}, f32[2,64,640]{2,1,0:T(8,128)}, u32[]{:S(2)}, u32[]{:S(2)}) %collective-permute-start.12) | collective-permute-done | bytes 327712 | tf_op jit(solution)/shard_map/ppermute | solution.py:330
  348.3 23.3 %consume.4 = (bf16[2,256,2560]{2,1,0:T(8,128)(2,1)}, bf16[2,256,2560]{2,1,0:T(8,128)(2,1)}, f32[16,64,1024]{2,1,0:T(8,128)}) custom-call(s32[1]{0:T(128)} %bitcast.4.me_ref, f32[2,64,640]{2,1,0:T(8,128)} %get-tuple-element.130.refs_0_, f32[2,64,640]{2,1,0:T(8,128)} %copy-done.35, f32[2,64,640]{2,1,0:T(8,128)} %copy-done.37, f32[2,64,640]{2,1,0:T(8,128)} %copy-done.38, ...), custom_call_target="tpu_custom_call" | custom-call | flops 15435038720 | bytes 18350080 | tf_op jit(solution)/shard_map/consume/pallas_call | solution.py:253
  372.8 30.5 %consume.5 = (bf16[2,256,2560]{2,1,0:T(8,128)(2,1)}, bf16[2,256,2560]{2,1,0:T(8,128)(2,1)}, f32[16,64,1024]{2,1,0:T(8,128)}) custom-call(s32[1]{0:T(128)} %bitcast.4.me_ref, f32[2,64,640]{2,1,0:T(8,128)} %get-tuple-element.114.refs_0_, f32[2,64,640]{2,1,0:T(8,128)} %copy-done.51, f32[2,64,640]{2,1,0:T(8,128)} %copy-done.53, f32[2,64,640]{2,1,0:T(8,128)} %copy-done.55, ...), custom_call_target="tpu_custom_call" | custom-call | flops 17448304640 | bytes 18350080 | tf_op jit(solution)/shard_map/consume/pallas_call | solution.py:253
  403.3 18.7 %contract.7 = (f32[32,4,8,640]{3,2,1,0:T(8,128)}, f32[32,4,8,640]{3,2,1,0:T(8,128)}) custom-call(s32[25]{0:T(128)} %pad_add_fusion.info_ref, bf16[512,64]{1,0:T(8,128)(2,1)} %copy.18.occ_ref, bf16[640,8,4096]{2,1,0:T(8,128)(2,1)} %x_ref.7), custom_call_target="tpu_custom_call" | custom-call | flops 2684354560 | bytes 10485760 | tf_op jit(solution)/shard_map/contract/pallas_call | solution.py:102
  427.8 18.6 %collective-permute-done.49.refs_1_ = f32[2,96,640]{2,1,0:T(8,128)S(1)} collective-permute-done((f32[2,96,640]{2,1,0:T(8,128)}, f32[2,96,640]{2,1,0:T(8,128)S(1)}, u32[]{:S(2)}, u32[]{:S(2)}) %collective-permute-start.49) | collective-permute-done | bytes 491552 | tf_op jit(solution)/shard_map/ppermute | solution.py:330
  446.5 14.2 %collective-permute-done.50.refs_2_ = f32[2,96,640]{2,1,0:T(8,128)S(1)} collective-permute-done((f32[2,96,640]{2,1,0:T(8,128)}, f32[2,96,640]{2,1,0:T(8,128)S(1)}, u32[]{:S(2)}, u32[]{:S(2)}) %collective-permute-start.50) | collective-permute-done | bytes 491552 | tf_op jit(solution)/shard_map/ppermute | solution.py:330
  471.3 24.8 %collective-permute-start.57 = (f32[2,96,640]{2,1,0:T(8,128)}, f32[2,96,640]{2,1,0:T(8,128)S(1)}, u32[]{:S(2)}, u32[]{:S(2)}) collective-permute-start(f32[2,96,640]{2,1,0:T(8,128)} %get-tuple-element.182), channel_id=1, source_target_pairs={{0,18},{2,16},{4,22},{6,20},{8,26},{10,24},{12,30},{14,28},{16,2},... | collective-permute-start | bytes 1474568 | tf_op jit(solution)/shard_map/ppermute | solution.py:330
  507.4 27.1 %collective-permute-done.57.refs_9_ = f32[2,96,640]{2,1,0:T(8,128)S(1)} collective-permute-done((f32[2,96,640]{2,1,0:T(8,128)}, f32[2,96,640]{2,1,0:T(8,128)S(1)}, u32[]{:S(2)}, u32[]{:S(2)}) %collective-permute-start.57) | collective-permute-done | bytes 491552 | tf_op jit(solution)/shard_map/ppermute | solution.py:330
  553.1 29.0 %collective-permute-start.34 = (f32[2,32,640]{2,1,0:T(8,128)}, f32[2,32,640]{2,1,0:T(8,128)S(1)}, u32[]{:S(2)}, u32[]{:S(2)}) collective-permute-start(f32[2,32,640]{2,1,0:T(8,128)} %get-tuple-element.156), channel_id=1, source_target_pairs={{0,2},{2,0},{4,6},{6,4},{8,10},{10,8},{12,14},{14,12},{16,18},{18,... | collective-permute-start | bytes 491528 | tf_op jit(solution)/shard_map/ppermute | solution.py:330
  584.5 16.0 %collective-permute-done.62.refs_14_ = f32[2,96,640]{2,1,0:T(8,128)} collective-permute-done((f32[2,96,640]{2,1,0:T(8,128)S(1)}, f32[2,96,640]{2,1,0:T(8,128)}, u32[]{:S(2)}, u32[]{:S(2)}) %collective-permute-start.62) | collective-permute-done | bytes 491552 | tf_op jit(solution)/shard_map/ppermute | solution.py:330
  648.2 42.5 %consume.6 = (bf16[2,384,2560]{2,1,0:T(8,128)(2,1)}, bf16[2,384,2560]{2,1,0:T(8,128)(2,1)}, f32[16,64,1024]{2,1,0:T(8,128)}) custom-call(s32[1]{0:T(128)} %bitcast.4.me_ref, f32[2,96,640]{2,1,0:T(8,128)} %get-tuple-element.173.refs_0_, f32[2,96,640]{2,1,0:T(8,128)} %copy-done.19, f32[2,96,640]{2,1,0:T(8,128)} %copy-done.20, f32[2,96,640]{2,1,0:T(8,128)} %copy-done.21, ...), custom_call_target="tpu_custom_call" | custom-call | flops 30702305280 | bytes 20971520 | tf_op jit(solution)/shard_map/consume/pallas_call | solution.py:253
  691.7 26.2 %consume.7 = f32[16,64,1024]{2,1,0:T(8,128)} custom-call(s32[1]{0:T(128)} %bitcast.4.me_ref, f32[2,32,640]{2,1,0:T(8,128)} %get-tuple-element.155.refs_0_, f32[2,32,640]{2,1,0:T(8,128)} %copy-done.1, f32[2,32,640]{2,1,0:T(8,128)} %copy-done.2, f32[2,32,640]{2,1,0:T(8,128)} %copy-done.3, f32[2,32,640]{2,1,0:T(8,128)} %copy-done.4, f32[2,32,640]{2,1,0:T(8,128)} %copy-done.5, ...), custom_call_target="tpu_custom_call" | custom-call | flops 10737418240 | bytes 15728640 | tf_op jit(solution)/shard_map/consume/pallas_call | solution.py:253
  731.1 11.6 %collective-permute-done.67 = f32[128,1024]{1,0:T(8,128)} collective-permute-done((f32[128,1024]{1,0:T(8,128)}, f32[128,1024]{1,0:T(8,128)}, u32[]{:S(2)}, u32[]{:S(2)}) %collective-permute-start.67) | collective-permute-done | bytes 524320 | tf_op jit(solution)/shard_map/ppermute | solution.py:275
  742.7 10.8 %collective-permute-done.66 = f32[128,1024]{1,0:T(8,128)} collective-permute-done((f32[128,1024]{1,0:T(8,128)S(1)}, f32[128,1024]{1,0:T(8,128)}, u32[]{:S(2)}, u32[]{:S(2)}) %collective-permute-start.66) | collective-permute-done | bytes 524320 | tf_op jit(solution)/shard_map/ppermute | solution.py:275
  (282 shorter events, 241.6 us)
Async XLA Ops:
  131.5 171.0 %collective-permute-start.2 = (f32[32,4,24,640]{3,2,1,0:T(8,128)}, f32[32,4,24,640]{3,2,1,0:T(8,128)}, u32[]{:S(2)}, u32[]{:S(2)}) collective-permute-start(f32[32,4,24,640]{3,2,1,0:T(8,128)} %get-tuple-element.110), channel_id=1, source_target_pairs={{0,1},{1,0},{2,3},{3,2},{4,5},{5,4},{6,7},{7,6},{8,9},{9,8},{10,11... | collective-permute-start | bytes 23592968 | tf_op jit(solution)/shard_map/ppermute | solution.py:323
  196.6 49.0 %collective-permute-start.30 = (f32[2,64,640]{2,1,0:T(8,128)}, f32[2,64,640]{2,1,0:T(8,128)S(1)}, u32[]{:S(2)}, u32[]{:S(2)}) collective-permute-start(f32[2,64,640]{2,1,0:T(8,128)} %get-tuple-element.143), channel_id=1, source_target_pairs={{0,26},{2,24},{4,30},{6,28},{8,18},{10,16},{12,22},{14,20},{16,10}... | collective-permute-start | bytes 983048 | tf_op jit(solution)/shard_map/ppermute | solution.py:330
  284.1 48.5 %collective-permute-start.11 = (f32[2,64,640]{2,1,0:T(8,128)S(1)}, f32[2,64,640]{2,1,0:T(8,128)}, u32[]{:S(2)}, u32[]{:S(2)}) collective-permute-start(f32[2,64,640]{2,1,0:T(8,128)S(1)} %copy-done.36), channel_id=1, source_target_pairs={{0,18},{2,16},{4,22},{6,20},{8,26},{10,24},{12,30},{14,28},{16,2},... | collective-permute-start | bytes 983048 | tf_op jit(solution)/shard_map/ppermute | solution.py:330
  302.6 42.9 %collective-permute-start.12 = (f32[2,64,640]{2,1,0:T(8,128)S(1)}, f32[2,64,640]{2,1,0:T(8,128)}, u32[]{:S(2)}, u32[]{:S(2)}) collective-permute-start(f32[2,64,640]{2,1,0:T(8,128)S(1)} %copy-done.34), channel_id=1, source_target_pairs={{0,20},{2,22},{4,16},{6,18},{8,28},{10,30},{12,24},{14,26},{16,4},... | collective-permute-start | bytes 983048 | tf_op jit(solution)/shard_map/ppermute | solution.py:330
  312.6 59.0 %collective-permute-start.13 = (f32[2,64,640]{2,1,0:T(8,128)S(1)}, f32[2,64,640]{2,1,0:T(8,128)S(1)}, u32[]{:S(2)}, u32[]{:S(2)}) collective-permute-start(f32[2,64,640]{2,1,0:T(8,128)S(1)} %copy-done.33), channel_id=1, source_target_pairs={{0,22},{2,20},{4,18},{6,16},{8,30},{10,28},{12,26},{14,24},{16,6},... | collective-permute-start | bytes 983048 | tf_op jit(solution)/shard_map/ppermute | solution.py:330
  315.3 56.2 %collective-permute-start.14 = (f32[2,64,640]{2,1,0:T(8,128)S(1)}, f32[2,64,640]{2,1,0:T(8,128)S(1)}, u32[]{:S(2)}, u32[]{:S(2)}) collective-permute-start(f32[2,64,640]{2,1,0:T(8,128)S(1)} %copy-done.32), channel_id=1, source_target_pairs={{0,24},{2,26},{4,28},{6,30},{8,16},{10,18},{12,20},{14,22},{16,8},... | collective-permute-start | bytes 983048 | tf_op jit(solution)/shard_map/ppermute | solution.py:330
  316.1 55.5 %collective-permute-start.15 = (f32[2,64,640]{2,1,0:T(8,128)S(1)}, f32[2,64,640]{2,1,0:T(8,128)S(1)}, u32[]{:S(2)}, u32[]{:S(2)}) collective-permute-start(f32[2,64,640]{2,1,0:T(8,128)S(1)} %copy-done.31), channel_id=1, source_target_pairs={{0,26},{2,24},{4,30},{6,28},{8,18},{10,16},{12,22},{14,20},{16,10}... | collective-permute-start | bytes 983048 | tf_op jit(solution)/shard_map/ppermute | solution.py:330
  422.0 124.7 %collective-permute-start.33 = (f32[32,4,8,640]{3,2,1,0:T(8,128)}, f32[32,4,8,640]{3,2,1,0:T(8,128)S(1)}, u32[]{:S(2)}, u32[]{:S(2)}) collective-permute-start(f32[32,4,8,640]{3,2,1,0:T(8,128)} %get-tuple-element.152), channel_id=1, source_target_pairs={{0,1},{1,0},{2,3},{3,2},{4,5},{5,4},{6,7},{7,6},{8,9},{9,8},{10,11... | collective-permute-start | bytes 7864328 | tf_op jit(solution)/shard_map/ppermute | solution.py:323
  460.7 42.6 %collective-permute-start.54 = (f32[2,96,640]{2,1,0:T(8,128)}, f32[2,96,640]{2,1,0:T(8,128)S(1)}, u32[]{:S(2)}, u32[]{:S(2)}) collective-permute-start(f32[2,96,640]{2,1,0:T(8,128)} %get-tuple-element.179), channel_id=1, source_target_pairs={{0,12},{2,14},{4,8},{6,10},{8,4},{10,6},{12,0},{14,2},{16,28},{18,... | collective-permute-start | bytes 1474568 | tf_op jit(solution)/shard_map/ppermute | solution.py:330
  460.8 42.6 %collective-permute-start.55 = (f32[2,96,640]{2,1,0:T(8,128)}, f32[2,96,640]{2,1,0:T(8,128)S(1)}, u32[]{:S(2)}, u32[]{:S(2)}) collective-permute-start(f32[2,96,640]{2,1,0:T(8,128)} %get-tuple-element.180), channel_id=1, source_target_pairs={{0,14},{2,12},{4,10},{6,8},{8,6},{10,4},{12,2},{14,0},{16,30},{18,... | collective-permute-start | bytes 1474568 | tf_op jit(solution)/shard_map/ppermute | solution.py:330
  463.5 42.5 %collective-permute-start.56 = (f32[2,96,640]{2,1,0:T(8,128)}, f32[2,96,640]{2,1,0:T(8,128)S(1)}, u32[]{:S(2)}, u32[]{:S(2)}) collective-permute-start(f32[2,96,640]{2,1,0:T(8,128)} %get-tuple-element.181), channel_id=1, source_target_pairs={{0,16},{2,18},{4,20},{6,22},{8,24},{10,26},{12,28},{14,30},{16,0},... | collective-permute-start | bytes 1474568 | tf_op jit(solution)/shard_map/ppermute | solution.py:330
  471.3 63.2 %collective-permute-start.57 = (f32[2,96,640]{2,1,0:T(8,128)}, f32[2,96,640]{2,1,0:T(8,128)S(1)}, u32[]{:S(2)}, u32[]{:S(2)}) collective-permute-start(f32[2,96,640]{2,1,0:T(8,128)} %get-tuple-element.182), channel_id=1, source_target_pairs={{0,18},{2,16},{4,22},{6,20},{8,26},{10,24},{12,30},{14,28},{16,2},... | collective-permute-start | bytes 1474568 | tf_op jit(solution)/shard_map/ppermute | solution.py:330
  503.3 42.5 %collective-permute-start.58 = (f32[2,96,640]{2,1,0:T(8,128)}, f32[2,96,640]{2,1,0:T(8,128)S(1)}, u32[]{:S(2)}, u32[]{:S(2)}) collective-permute-start(f32[2,96,640]{2,1,0:T(8,128)} %get-tuple-element.183), channel_id=1, source_target_pairs={{0,20},{2,22},{4,16},{6,18},{8,28},{10,30},{12,24},{14,26},{16,4},... | collective-permute-start | bytes 1474568 | tf_op jit(solution)/shard_map/ppermute | solution.py:330
  503.3 49.8 %collective-permute-start.59 = (f32[2,96,640]{2,1,0:T(8,128)}, f32[2,96,640]{2,1,0:T(8,128)}, u32[]{:S(2)}, u32[]{:S(2)}) collective-permute-start(f32[2,96,640]{2,1,0:T(8,128)} %get-tuple-element.184), channel_id=1, source_target_pairs={{0,22},{2,20},{4,18},{6,16},{8,30},{10,28},{12,26},{14,24},{16,6},... | collective-permute-start | bytes 1474568 | tf_op jit(solution)/shard_map/ppermute | solution.py:330
  506.0 76.2 %collective-permute-start.60 = (f32[2,96,640]{2,1,0:T(8,128)}, f32[2,96,640]{2,1,0:T(8,128)}, u32[]{:S(2)}, u32[]{:S(2)}) collective-permute-start(f32[2,96,640]{2,1,0:T(8,128)} %get-tuple-element.185), channel_id=1, source_target_pairs={{0,24},{2,26},{4,28},{6,30},{8,16},{10,18},{12,20},{14,22},{16,8},... | collective-permute-start | bytes 1474568 | tf_op jit(solution)/shard_map/ppermute | solution.py:330
  534.5 48.3 %collective-permute-start.61 = (f32[2,96,640]{2,1,0:T(8,128)S(1)}, f32[2,96,640]{2,1,0:T(8,128)}, u32[]{:S(2)}, u32[]{:S(2)}) collective-permute-start(f32[2,96,640]{2,1,0:T(8,128)S(1)} %copy-done.18), channel_id=1, source_target_pairs={{0,26},{2,24},{4,30},{6,28},{8,18},{10,16},{12,22},{14,20},{16,10}... | collective-permute-start | bytes 1474568 | tf_op jit(solution)/shard_map/ppermute | solution.py:330
  545.8 54.6 %collective-permute-start.62 = (f32[2,96,640]{2,1,0:T(8,128)S(1)}, f32[2,96,640]{2,1,0:T(8,128)}, u32[]{:S(2)}, u32[]{:S(2)}) collective-permute-start(f32[2,96,640]{2,1,0:T(8,128)S(1)} %copy-done.17), channel_id=1, source_target_pairs={{0,28},{2,30},{4,24},{6,26},{8,20},{10,22},{12,16},{14,18},{16,12}... | collective-permute-start | bytes 1474568 | tf_op jit(solution)/shard_map/ppermute | solution.py:330
  546.7 54.0 %collective-permute-start.63 = (f32[2,96,640]{2,1,0:T(8,128)S(1)}, f32[2,96,640]{2,1,0:T(8,128)}, u32[]{:S(2)}, u32[]{:S(2)}) collective-permute-start(f32[2,96,640]{2,1,0:T(8,128)S(1)} %copy-done.16), channel_id=1, source_target_pairs={{0,30},{2,28},{4,26},{6,24},{8,22},{10,20},{12,18},{14,16},{16,14}... | collective-permute-start | bytes 1474568 | tf_op jit(solution)/shard_map/ppermute | solution.py:330
  553.1 58.1 %collective-permute-start.34 = (f32[2,32,640]{2,1,0:T(8,128)}, f32[2,32,640]{2,1,0:T(8,128)S(1)}, u32[]{:S(2)}, u32[]{:S(2)}) collective-permute-start(f32[2,32,640]{2,1,0:T(8,128)} %get-tuple-element.156), channel_id=1, source_target_pairs={{0,2},{2,0},{4,6},{6,4},{8,10},{10,8},{12,14},{14,12},{16,18},{18,... | collective-permute-start | bytes 491528 | tf_op jit(solution)/shard_map/ppermute | solution.py:330
  628.2 62.6 %collective-permute-start.44 = (f32[2,32,640]{2,1,0:T(8,128)}, f32[2,32,640]{2,1,0:T(8,128)S(1)}, u32[]{:S(2)}, u32[]{:S(2)}) collective-permute-start(f32[2,32,640]{2,1,0:T(8,128)} %get-tuple-element.166), channel_id=1, source_target_pairs={{0,22},{2,20},{4,18},{6,16},{8,30},{10,28},{12,26},{14,24},{16,6},... | collective-permute-start | bytes 491528 | tf_op jit(solution)/shard_map/ppermute | solution.py:330
  631.8 59.0 %collective-permute-start.45 = (f32[2,32,640]{2,1,0:T(8,128)}, f32[2,32,640]{2,1,0:T(8,128)S(1)}, u32[]{:S(2)}, u32[]{:S(2)}) collective-permute-start(f32[2,32,640]{2,1,0:T(8,128)} %get-tuple-element.167), channel_id=1, source_target_pairs={{0,24},{2,26},{4,28},{6,30},{8,16},{10,18},{12,20},{14,22},{16,8},... | collective-permute-start | bytes 491528 | tf_op jit(solution)/shard_map/ppermute | solution.py:330
  632.0 58.8 %collective-permute-start.46 = (f32[2,32,640]{2,1,0:T(8,128)}, f32[2,32,640]{2,1,0:T(8,128)S(1)}, u32[]{:S(2)}, u32[]{:S(2)}) collective-permute-start(f32[2,32,640]{2,1,0:T(8,128)} %get-tuple-element.168), channel_id=1, source_target_pairs={{0,26},{2,24},{4,30},{6,28},{8,18},{10,16},{12,22},{14,20},{16,10}... | collective-permute-start | bytes 491528 | tf_op jit(solution)/shard_map/ppermute | solution.py:330
  640.7 50.2 %collective-permute-start.47 = (f32[2,32,640]{2,1,0:T(8,128)}, f32[2,32,640]{2,1,0:T(8,128)S(1)}, u32[]{:S(2)}, u32[]{:S(2)}) collective-permute-start(f32[2,32,640]{2,1,0:T(8,128)} %get-tuple-element.169), channel_id=1, source_target_pairs={{0,28},{2,30},{4,24},{6,26},{8,20},{10,22},{12,16},{14,18},{16,12}... | collective-permute-start | bytes 491528 | tf_op jit(solution)/shard_map/ppermute | solution.py:330
  645.6 45.3 %collective-permute-start.48 = (f32[2,32,640]{2,1,0:T(8,128)}, f32[2,32,640]{2,1,0:T(8,128)S(1)}, u32[]{:S(2)}, u32[]{:S(2)}) collective-permute-start(f32[2,32,640]{2,1,0:T(8,128)} %get-tuple-element.170), channel_id=1, source_target_pairs={{0,30},{2,28},{4,26},{6,24},{8,22},{10,20},{12,18},{14,16},{16,14}... | collective-permute-start | bytes 491528 | tf_op jit(solution)/shard_map/ppermute | solution.py:330
  (114 other events, 5840.1 us)

commit v3 on v1

--- a/solution.py
+++ b/solution.py
@@ -52,9 +52,9 @@
 
     @pl.when(pl.program_id(0) == 0)
     def _():
-        spread = lax.broadcasted_iota(jnp.int32, (tall, occ), 0) // octet == lax.broadcasted_iota(
-            jnp.int32, (tall, occ), 1
-        )
+        first = (1 - info_ref[0]) * half
+        orbital = (lax.broadcasted_iota(jnp.int32, (tall, occ), 0) // octet + first) % occ
+        spread = orbital == lax.broadcasted_iota(jnp.int32, (tall, occ), 1)
         spread = spread.astype(jnp.bfloat16)
         tile = lax.broadcasted_iota(jnp.int32, (BS, wide), 1) % BS == lax.broadcasted_iota(jnp.int32, (BS, wide), 0)
         tile = tile.astype(jnp.bfloat16)
@@ -80,18 +80,17 @@
         return 0
 
     lax.fori_loop(0, aux_rows // 128, turn, 0)
-    col = info_ref[0]
-    for h, out_ref in ((1 - col, other_ref), (col, mine_ref)):
-        out_ref[...] = jnp.zeros_like(out_ref)
-
-        def one(s, _):
-            w = w_ref[s, pl.ds(pl.multiple_of(h * half * octet, 16), half * octet)]
-            piece = lax.dot_general(w, xt_ref[s], (((1,), (1,)), ((), ())), **f32)
-            b = info_ref[1 + s]
-            out_ref[:, b] = out_ref[:, b] + piece.reshape(half, octet, aux_rows)
-            return 0
-
-        lax.fori_loop(0, slots, one, 0)
+    other_ref[...] = jnp.zeros_like(other_ref)
+    mine_ref[...] = jnp.zeros_like(mine_ref)
+
+    def one(s, _):
+        piece = lax.dot_general(w_ref[s], xt_ref[s], (((1,), (1,)), ((), ())), **f32)
+        b = info_ref[1 + s]
+        other_ref[:, b] = other_ref[:, b] + piece[: half * octet].reshape(half, octet, aux_rows)
+        mine_ref[:, b] = mine_ref[:, b] + piece[half * octet :].reshape(half, octet, aux_rows)
+        return 0
+
+    lax.fori_loop(0, slots, one, 0)
 
 
 def contract(info, occupied, integrals, lo, m, row_blocks):
@@ -308,10 +307,13 @@
     starts = tuple(sum(sizes[:c]) for c in range(len(sizes)))
     count = len(sizes)
     arrived, earlier, total = [], [], None
-
-    def use(c, me_array):
-        last = c == count - 1
-        return consume(me_array, arrived[c], metric, earlier, total, n_row, nbf, starts[: c + 1], sizes[: c + 1], last)
+    order = (*range(count - 2), count - 1, count - 2)
+
+    def use(k, me_array):
+        los, ms = [tuple(v[c] for c in order[: k + 1]) for v in (starts, sizes)]
+        return consume(
+            me_array, arrived[order[k]], metric, earlier, total, n_row, nbf, los, ms, k == count - 1
+        )
 
     for c in range(count):
         if c == count - 1:

time: 770 us -> 764 us (level)
  waiting for transfers between devices: 173 us -> 199 us
  starting transfers between devices: 312 us -> 293 us
  Pallas kernels: 270 us -> 255 us
    ppermute x60, waiting for transfers between devices: 117 us -> 142 us  [body(): lax.ppermute(pieces[d], ('aux', 'row'), pairs)]
    ppermute x60, starting transfers between devices: 303 us -> 281 us  [body(): lax.ppermute(pieces[d], ('aux', 'row'), pairs)]
    pallas_call x4, Pallas kernels: 114 us -> 103 us  [contract(): pl.pallas_call(contract_kernel, grid_spec=pltpu.PrefetchScalarGridSpec(nu...]
  transfers between devices with their start and end apart: 71 -> 71, of which waited for: 26 -> 28; matrix products, arithmetic and copies ran while one was open for 0% -> 0% of each run, Pallas kernels for 17% -> 10%
where the time goes in v3:
time: 764 us
  starting transfers between devices  293 us (38%)
  Pallas kernels  255 us (33%)
  waiting for transfers between devices  199 us (26%)
  local copies, waits for them, and re-layouts  9.5 us (1%)
    ppermute x60, starting transfers between devices, body(): lax.ppermute(pieces[d], ('aux', 'row'), pairs)  281 us
    ppermute x60, waiting for transfers between devices, body(): lax.ppermute(pieces[d], ('aux', 'row'), pairs)  142 us
    pallas_call x4, Pallas kernels, consume(): pl.pallas_call(functools.partial(consume_kernel, n_row=n_row, starts=star...  124 us
    pallas_call x4, Pallas kernels, contract(): pl.pallas_call(contract_kernel, grid_spec=pltpu.PrefetchScalarGridSpec(nu...  103 us
    ppermute x6, waiting for transfers between devices, swap_sum(): own = own + lax.ppermute(given, axis, [(s, s ^ d) for s in range(n)])  31.5 us
    pallas_call x4, Pallas kernels, combine(): pl.pallas_call(combine_kernel, in_specs=[pl.BlockSpec(memory_space=pltpu....  27.5 us
    ppermute x4, waiting for transfers between devices, body(): got = lax.ppermute(other, 'col', [(0, 1), (1, 0)])  21.4 us
  transfers between devices with their start and end apart: 71, of which 28 were waited for; matrix products, arithmetic and copies ran while one was open for 0% of the time, Pallas kernels for 10%

profile of v3, /device:TPU:0, one launch (start us, length us, event | category | flops | bytes accessed | tf_op | source)
XLA Modules:
  0.0 763.6 jit_solution(11071363076263534071)
XLA Ops:
  3.7 25.7 %contract.4 = (f32[32,4,16,640]{3,2,1,0:T(8,128)}, f32[32,4,16,640]{3,2,1,0:T(8,128)}) custom-call(s32[25]{0:T(128)} %pad_add_fusion.info_ref, bf16[512,64]{1,0:T(8,128)(2,1)} %copy.18.occ_ref, bf16[640,8,4096]{2,1,0:T(8,128)(2,1)} %x_ref.7), custom_call_target="tpu_custom_call" | custom-call | flops 5368709120 | bytes 20971520 | tf_op jit(solution)/shard_map/contract/pallas_call | solution.py:101
  45.3 33.9 %contract.5 = (f32[32,4,24,640]{3,2,1,0:T(8,128)}, f32[32,4,24,640]{3,2,1,0:T(8,128)}) custom-call(s32[25]{0:T(128)} %pad_add_fusion.info_ref, bf16[512,64]{1,0:T(8,128)(2,1)} %copy.18.occ_ref, bf16[640,8,4096]{2,1,0:T(8,128)(2,1)} %x_ref.7), custom_call_target="tpu_custom_call" | custom-call | flops 8053063680 | bytes 31457280 | tf_op jit(solution)/shard_map/contract/pallas_call | solution.py:101
  79.3 12.7 %collective-permute-done.1 = f32[32,4,24,640]{3,2,1,0:T(8,128)} collective-permute-done((f32[32,4,24,640]{3,2,1,0:T(8,128)}, f32[32,4,24,640]{3,2,1,0:T(8,128)}, u32[]{:S(2)}, u32[]{:S(2)}) %collective-permute-start.1) | collective-permute-done | bytes 7864352 | tf_op jit(solution)/shard_map/ppermute | solution.py:324
  101.4 25.8 %contract.6 = (f32[32,4,16,640]{3,2,1,0:T(8,128)}, f32[32,4,16,640]{3,2,1,0:T(8,128)}) custom-call(s32[25]{0:T(128)} %pad_add_fusion.info_ref, bf16[512,64]{1,0:T(8,128)(2,1)} %copy.18.occ_ref, bf16[640,8,4096]{2,1,0:T(8,128)(2,1)} %x_ref.7), custom_call_target="tpu_custom_call" | custom-call | flops 5368709120 | bytes 20971520 | tf_op jit(solution)/shard_map/contract/pallas_call | solution.py:101
  162.3 19.8 %collective-permute-start.11 = (f32[2,64,640]{2,1,0:T(8,128)S(1)}, f32[2,64,640]{2,1,0:T(8,128)S(1)}, u32[]{:S(2)}, u32[]{:S(2)}) collective-permute-start(f32[2,64,640]{2,1,0:T(8,128)S(1)} %copy-done.37), channel_id=1, source_target_pairs={{0,18},{2,16},{4,22},{6,20},{8,26},{10,24},{12,30},{14,28},{16,2},... | collective-permute-start | bytes 983048 | tf_op jit(solution)/shard_map/ppermute | solution.py:331
  192.0 20.6 %collective-permute-start.15 = (f32[2,64,640]{2,1,0:T(8,128)S(1)}, f32[2,64,640]{2,1,0:T(8,128)S(1)}, u32[]{:S(2)}, u32[]{:S(2)}) collective-permute-start(f32[2,64,640]{2,1,0:T(8,128)S(1)} %copy-done.28), channel_id=1, source_target_pairs={{0,26},{2,24},{4,30},{6,28},{8,18},{10,16},{12,22},{14,20},{16,10}... | collective-permute-start | bytes 983048 | tf_op jit(solution)/shard_map/ppermute | solution.py:331
  224.7 21.2 %collective-permute-done.16.refs_14_ = f32[2,64,640]{2,1,0:T(8,128)S(1)} collective-permute-done((f32[2,64,640]{2,1,0:T(8,128)S(1)}, f32[2,64,640]{2,1,0:T(8,128)S(1)}, u32[]{:S(2)}, u32[]{:S(2)}) %collective-permute-start.16) | collective-permute-done | bytes 327712 | tf_op jit(solution)/shard_map/ppermute | solution.py:331
  246.6 23.2 %consume.4 = (bf16[2,256,2560]{2,1,0:T(8,128)(2,1)}, bf16[2,256,2560]{2,1,0:T(8,128)(2,1)}, f32[16,64,1024]{2,1,0:T(8,128)}) custom-call(s32[1]{0:T(128)} %bitcast.4.me_ref, f32[2,64,640]{2,1,0:T(8,128)} %get-tuple-element.114.refs_0_, f32[2,64,640]{2,1,0:T(8,128)} %copy-done.31, f32[2,64,640]{2,1,0:T(8,128)} %copy-done.32, f32[2,64,640]{2,1,0:T(8,128)} %copy-done.33, ...), custom_call_target="tpu_custom_call" | custom-call | flops 15435038720 | bytes 18350080 | tf_op jit(solution)/shard_map/consume/pallas_call | solution.py:252
  269.8 17.6 %contract.7 = (f32[32,4,8,640]{3,2,1,0:T(8,128)}, f32[32,4,8,640]{3,2,1,0:T(8,128)}) custom-call(s32[25]{0:T(128)} %pad_add_fusion.info_ref, bf16[512,64]{1,0:T(8,128)(2,1)} %copy.18.occ_ref, bf16[640,8,4096]{2,1,0:T(8,128)(2,1)} %x_ref.7), custom_call_target="tpu_custom_call" | custom-call | flops 2684354560 | bytes 10485760 | tf_op jit(solution)/shard_map/contract/pallas_call | solution.py:101
  297.1 18.5 %collective-permute-done.34.refs_1_ = f32[2,96,640]{2,1,0:T(8,128)S(1)} collective-permute-done((f32[2,96,640]{2,1,0:T(8,128)}, f32[2,96,640]{2,1,0:T(8,128)S(1)}, u32[]{:S(2)}, u32[]{:S(2)}) %collective-permute-start.34) | collective-permute-done | bytes 491552 | tf_op jit(solution)/shard_map/ppermute | solution.py:331
  315.6 14.4 %collective-permute-done.35.refs_2_ = f32[2,96,640]{2,1,0:T(8,128)S(1)} collective-permute-done((f32[2,96,640]{2,1,0:T(8,128)}, f32[2,96,640]{2,1,0:T(8,128)S(1)}, u32[]{:S(2)}, u32[]{:S(2)}) %collective-permute-start.35) | collective-permute-done | bytes 491552 | tf_op jit(solution)/shard_map/ppermute | solution.py:331
  340.2 24.6 %collective-permute-start.42 = (f32[2,96,640]{2,1,0:T(8,128)}, f32[2,96,640]{2,1,0:T(8,128)S(1)}, u32[]{:S(2)}, u32[]{:S(2)}) collective-permute-start(f32[2,96,640]{2,1,0:T(8,128)} %get-tuple-element.163), channel_id=1, source_target_pairs={{0,18},{2,16},{4,22},{6,20},{8,26},{10,24},{12,30},{14,28},{16,2},... | collective-permute-start | bytes 1474568 | tf_op jit(solution)/shard_map/ppermute | solution.py:331
  377.6 30.6 %collective-permute-start.46 = (f32[2,96,640]{2,1,0:T(8,128)}, f32[2,96,640]{2,1,0:T(8,128)S(1)}, u32[]{:S(2)}, u32[]{:S(2)}) collective-permute-start(f32[2,96,640]{2,1,0:T(8,128)} %get-tuple-element.167), channel_id=1, source_target_pairs={{0,26},{2,24},{4,30},{6,28},{8,18},{10,16},{12,22},{14,20},{16,10}... | collective-permute-start | bytes 1474568 | tf_op jit(solution)/shard_map/ppermute | solution.py:331
  417.8 35.9 %collective-permute-start.19 = (f32[2,64,640]{2,1,0:T(8,128)}, f32[2,64,640]{2,1,0:T(8,128)S(1)}, u32[]{:S(2)}, u32[]{:S(2)}) collective-permute-start(f32[2,64,640]{2,1,0:T(8,128)} %get-tuple-element.137), channel_id=1, source_target_pairs={{0,2},{2,0},{4,6},{6,4},{8,10},{10,8},{12,14},{14,12},{16,18},{18,... | collective-permute-start | bytes 983048 | tf_op jit(solution)/shard_map/ppermute | solution.py:331
  466.3 11.1 %collective-permute-start.22 = (f32[2,64,640]{2,1,0:T(8,128)}, f32[2,64,640]{2,1,0:T(8,128)S(1)}, u32[]{:S(2)}, u32[]{:S(2)}) collective-permute-start(f32[2,64,640]{2,1,0:T(8,128)} %get-tuple-element.140), channel_id=1, source_target_pairs={{0,8},{2,10},{4,12},{6,14},{8,0},{10,2},{12,4},{14,6},{16,24},{18,... | collective-permute-start | bytes 983048 | tf_op jit(solution)/shard_map/ppermute | solution.py:331
  477.4 11.2 %collective-permute-start.23 = (f32[2,64,640]{2,1,0:T(8,128)}, f32[2,64,640]{2,1,0:T(8,128)S(1)}, u32[]{:S(2)}, u32[]{:S(2)}) collective-permute-start(f32[2,64,640]{2,1,0:T(8,128)} %get-tuple-element.141), channel_id=1, source_target_pairs={{0,10},{2,8},{4,14},{6,12},{8,2},{10,0},{12,6},{14,4},{16,26},{18,... | collective-permute-start | bytes 983048 | tf_op jit(solution)/shard_map/ppermute | solution.py:331
  499.6 18.0 %collective-permute-start.27 = (f32[2,64,640]{2,1,0:T(8,128)}, f32[2,64,640]{2,1,0:T(8,128)}, u32[]{:S(2)}, u32[]{:S(2)}) collective-permute-start(f32[2,64,640]{2,1,0:T(8,128)} %get-tuple-element.145), channel_id=1, source_target_pairs={{0,18},{2,16},{4,22},{6,20},{8,26},{10,24},{12,30},{14,28},{16,2},... | collective-permute-start | bytes 983048 | tf_op jit(solution)/shard_map/ppermute | solution.py:331
  524.8 11.9 %collective-permute-start.50 = (f32[2,32,640]{2,1,0:T(8,128)}, f32[2,32,640]{2,1,0:T(8,128)}, u32[]{:S(2)}, u32[]{:S(2)}) collective-permute-start(f32[2,32,640]{2,1,0:T(8,128)} %get-tuple-element.175), channel_id=1, source_target_pairs={{0,4},{2,6},{4,0},{6,2},{8,12},{10,14},{12,8},{14,10},{16,20},{18,... | collective-permute-start | bytes 491528 | tf_op jit(solution)/shard_map/ppermute | solution.py:331
  539.4 10.4 %collective-permute-done.28.refs_10_ = f32[2,64,640]{2,1,0:T(8,128)} collective-permute-done((f32[2,64,640]{2,1,0:T(8,128)}, f32[2,64,640]{2,1,0:T(8,128)}, u32[]{:S(2)}, u32[]{:S(2)}) %collective-permute-start.28) | collective-permute-done | bytes 327712 | tf_op jit(solution)/shard_map/ppermute | solution.py:331
  588.7 44.0 %consume.5 = (bf16[2,384,2560]{2,1,0:T(8,128)(2,1)}, bf16[2,384,2560]{2,1,0:T(8,128)(2,1)}, f32[16,64,1024]{2,1,0:T(8,128)}) custom-call(s32[1]{0:T(128)} %bitcast.4.me_ref, f32[2,96,640]{2,1,0:T(8,128)} %get-tuple-element.154.refs_0_, f32[2,96,640]{2,1,0:T(8,128)} %copy-done.1, f32[2,96,640]{2,1,0:T(8,128)} %copy-done.2, f32[2,96,640]{2,1,0:T(8,128)} %copy-done.3, ...), custom_call_target="tpu_custom_call" | custom-call | flops 27682406400 | bytes 20971520 | tf_op jit(solution)/shard_map/consume/pallas_call | solution.py:252
  645.3 23.5 %consume.6 = (bf16[2,128,2560]{2,1,0:T(8,128)(2,1)}, bf16[2,128,2560]{2,1,0:T(8,128)(2,1)}, f32[16,64,1024]{2,1,0:T(8,128)}) custom-call(s32[1]{0:T(128)} %bitcast.4.me_ref, f32[2,32,640]{2,1,0:T(8,128)} %get-tuple-element.173.refs_0_, f32[2,32,640]{2,1,0:T(8,128)} %collective-permute-done.49.refs_1_, f32[2,32,640]{2,1,0:T(8,128)} %collective-permute-done.50.refs_2_, ...), custom_call_target="tpu_custom_call" | custom-call | flops 9730785280 | bytes 15728640 | tf_op jit(solution)/shard_map/consume/pallas_call | solution.py:252
  674.5 33.7 %consume.7 = f32[16,64,1024]{2,1,0:T(8,128)} custom-call(s32[1]{0:T(128)} %bitcast.4.me_ref, f32[2,64,640]{2,1,0:T(8,128)} %get-tuple-element.136.refs_0_, f32[2,64,640]{2,1,0:T(8,128)} %copy-done.21, f32[2,64,640]{2,1,0:T(8,128)} %copy-done.22, f32[2,64,640]{2,1,0:T(8,128)} %copy-done.23, f32[2,64,640]{2,1,0:T(8,128)} %copy-done.24, ...), custom_call_target="tpu_custom_call" | custom-call | flops 21474836480 | bytes 18350080 | tf_op jit(solution)/shard_map/consume/pallas_call | solution.py:252
  721.3 11.6 %collective-permute-done.67 = f32[128,1024]{1,0:T(8,128)} collective-permute-done((f32[128,1024]{1,0:T(8,128)}, f32[128,1024]{1,0:T(8,128)}, u32[]{:S(2)}, u32[]{:S(2)}) %collective-permute-start.67) | collective-permute-done | bytes 524320 | tf_op jit(solution)/shard_map/ppermute | solution.py:274
  733.0 10.3 %collective-permute-done.65 = f32[128,1024]{1,0:T(8,128)} collective-permute-done((f32[128,1024]{1,0:T(8,128)S(1)}, f32[128,1024]{1,0:T(8,128)}, u32[]{:S(2)}, u32[]{:S(2)}) %collective-permute-start.65) | collective-permute-done | bytes 524320 | tf_op jit(solution)/shard_map/ppermute | solution.py:274
  (266 shorter events, 252.8 us)
Async XLA Ops:
  127.2 86.8 %collective-permute-start.2 = (f32[32,4,16,640]{3,2,1,0:T(8,128)}, f32[32,4,16,640]{3,2,1,0:T(8,128)}, u32[]{:S(2)}, u32[]{:S(2)}) collective-permute-start(f32[32,4,16,640]{3,2,1,0:T(8,128)} %get-tuple-element.110), channel_id=1, source_target_pairs={{0,1},{1,0},{2,3},{3,2},{4,5},{5,4},{6,7},{7,6},{8,9},{9,8},{10,11... | collective-permute-start | bytes 15728648 | tf_op jit(solution)/shard_map/ppermute | solution.py:324
  185.0 39.7 %collective-permute-start.13 = (f32[2,64,640]{2,1,0:T(8,128)S(1)}, f32[2,64,640]{2,1,0:T(8,128)}, u32[]{:S(2)}, u32[]{:S(2)}) collective-permute-start(f32[2,64,640]{2,1,0:T(8,128)S(1)} %copy-done.30), channel_id=1, source_target_pairs={{0,22},{2,20},{4,18},{6,16},{8,30},{10,28},{12,26},{14,24},{16,6},... | collective-permute-start | bytes 983048 | tf_op jit(solution)/shard_map/ppermute | solution.py:331
  287.3 230.3 %collective-permute-start.18 = (f32[32,4,8,640]{3,2,1,0:T(8,128)}, f32[32,4,8,640]{3,2,1,0:T(8,128)S(1)}, u32[]{:S(2)}, u32[]{:S(2)}) collective-permute-start(f32[32,4,8,640]{3,2,1,0:T(8,128)} %get-tuple-element.133), channel_id=1, source_target_pairs={{0,1},{1,0},{2,3},{3,2},{4,5},{5,4},{6,7},{7,6},{8,9},{9,8},{10,11... | collective-permute-start | bytes 7864328 | tf_op jit(solution)/shard_map/ppermute | solution.py:324
  293.6 36.4 %collective-permute-start.35 = (f32[2,96,640]{2,1,0:T(8,128)}, f32[2,96,640]{2,1,0:T(8,128)S(1)}, u32[]{:S(2)}, u32[]{:S(2)}) collective-permute-start(f32[2,96,640]{2,1,0:T(8,128)} %get-tuple-element.156), channel_id=1, source_target_pairs={{0,4},{2,6},{4,0},{6,2},{8,12},{10,14},{12,8},{14,10},{16,20},{18,... | collective-permute-start | bytes 1474568 | tf_op jit(solution)/shard_map/ppermute | solution.py:331
  296.0 36.5 %collective-permute-start.37 = (f32[2,96,640]{2,1,0:T(8,128)}, f32[2,96,640]{2,1,0:T(8,128)S(1)}, u32[]{:S(2)}, u32[]{:S(2)}) collective-permute-start(f32[2,96,640]{2,1,0:T(8,128)} %get-tuple-element.158), channel_id=1, source_target_pairs={{0,8},{2,10},{4,12},{6,14},{8,0},{10,2},{12,4},{14,6},{16,24},{18,... | collective-permute-start | bytes 1474568 | tf_op jit(solution)/shard_map/ppermute | solution.py:331
  330.0 42.7 %collective-permute-start.39 = (f32[2,96,640]{2,1,0:T(8,128)}, f32[2,96,640]{2,1,0:T(8,128)S(1)}, u32[]{:S(2)}, u32[]{:S(2)}) collective-permute-start(f32[2,96,640]{2,1,0:T(8,128)} %get-tuple-element.160), channel_id=1, source_target_pairs={{0,12},{2,14},{4,8},{6,10},{8,4},{10,6},{12,0},{14,2},{16,28},{18,... | collective-permute-start | bytes 1474568 | tf_op jit(solution)/shard_map/ppermute | solution.py:331
  330.1 42.5 %collective-permute-start.40 = (f32[2,96,640]{2,1,0:T(8,128)}, f32[2,96,640]{2,1,0:T(8,128)S(1)}, u32[]{:S(2)}, u32[]{:S(2)}) collective-permute-start(f32[2,96,640]{2,1,0:T(8,128)} %get-tuple-element.161), channel_id=1, source_target_pairs={{0,14},{2,12},{4,10},{6,8},{8,6},{10,4},{12,2},{14,0},{16,30},{18,... | collective-permute-start | bytes 1474568 | tf_op jit(solution)/shard_map/ppermute | solution.py:331
  332.6 42.2 %collective-permute-start.41 = (f32[2,96,640]{2,1,0:T(8,128)}, f32[2,96,640]{2,1,0:T(8,128)S(1)}, u32[]{:S(2)}, u32[]{:S(2)}) collective-permute-start(f32[2,96,640]{2,1,0:T(8,128)} %get-tuple-element.162), channel_id=1, source_target_pairs={{0,16},{2,18},{4,20},{6,22},{8,24},{10,26},{12,28},{14,30},{16,0},... | collective-permute-start | bytes 1474568 | tf_op jit(solution)/shard_map/ppermute | solution.py:331
  340.2 37.4 %collective-permute-start.42 = (f32[2,96,640]{2,1,0:T(8,128)}, f32[2,96,640]{2,1,0:T(8,128)S(1)}, u32[]{:S(2)}, u32[]{:S(2)}) collective-permute-start(f32[2,96,640]{2,1,0:T(8,128)} %get-tuple-element.163), channel_id=1, source_target_pairs={{0,18},{2,16},{4,22},{6,20},{8,26},{10,24},{12,30},{14,28},{16,2},... | collective-permute-start | bytes 1474568 | tf_op jit(solution)/shard_map/ppermute | solution.py:331
  372.6 42.2 %collective-permute-start.43 = (f32[2,96,640]{2,1,0:T(8,128)}, f32[2,96,640]{2,1,0:T(8,128)S(1)}, u32[]{:S(2)}, u32[]{:S(2)}) collective-permute-start(f32[2,96,640]{2,1,0:T(8,128)} %get-tuple-element.164), channel_id=1, source_target_pairs={{0,20},{2,22},{4,16},{6,18},{8,28},{10,30},{12,24},{14,26},{16,4},... | collective-permute-start | bytes 1474568 | tf_op jit(solution)/shard_map/ppermute | solution.py:331
  372.6 42.2 %collective-permute-start.44 = (f32[2,96,640]{2,1,0:T(8,128)}, f32[2,96,640]{2,1,0:T(8,128)S(1)}, u32[]{:S(2)}, u32[]{:S(2)}) collective-permute-start(f32[2,96,640]{2,1,0:T(8,128)} %get-tuple-element.165), channel_id=1, source_target_pairs={{0,22},{2,20},{4,18},{6,16},{8,30},{10,28},{12,26},{14,24},{16,6},... | collective-permute-start | bytes 1474568 | tf_op jit(solution)/shard_map/ppermute | solution.py:331
  374.8 43.0 %collective-permute-start.45 = (f32[2,96,640]{2,1,0:T(8,128)}, f32[2,96,640]{2,1,0:T(8,128)S(1)}, u32[]{:S(2)}, u32[]{:S(2)}) collective-permute-start(f32[2,96,640]{2,1,0:T(8,128)} %get-tuple-element.166), channel_id=1, source_target_pairs={{0,24},{2,26},{4,28},{6,30},{8,16},{10,18},{12,20},{14,22},{16,8},... | collective-permute-start | bytes 1474568 | tf_op jit(solution)/shard_map/ppermute | solution.py:331
  377.6 76.2 %collective-permute-start.46 = (f32[2,96,640]{2,1,0:T(8,128)}, f32[2,96,640]{2,1,0:T(8,128)S(1)}, u32[]{:S(2)}, u32[]{:S(2)}) collective-permute-start(f32[2,96,640]{2,1,0:T(8,128)} %get-tuple-element.167), channel_id=1, source_target_pairs={{0,26},{2,24},{4,30},{6,28},{8,18},{10,16},{12,22},{14,20},{16,10}... | collective-permute-start | bytes 1474568 | tf_op jit(solution)/shard_map/ppermute | solution.py:331
  414.8 49.0 %collective-permute-start.47 = (f32[2,96,640]{2,1,0:T(8,128)}, f32[2,96,640]{2,1,0:T(8,128)S(1)}, u32[]{:S(2)}, u32[]{:S(2)}) collective-permute-start(f32[2,96,640]{2,1,0:T(8,128)} %get-tuple-element.168), channel_id=1, source_target_pairs={{0,28},{2,30},{4,24},{6,26},{8,20},{10,22},{12,16},{14,18},{16,12}... | collective-permute-start | bytes 1474568 | tf_op jit(solution)/shard_map/ppermute | solution.py:331
  414.9 51.4 %collective-permute-start.48 = (f32[2,96,640]{2,1,0:T(8,128)}, f32[2,96,640]{2,1,0:T(8,128)S(1)}, u32[]{:S(2)}, u32[]{:S(2)}) collective-permute-start(f32[2,96,640]{2,1,0:T(8,128)} %get-tuple-element.169), channel_id=1, source_target_pairs={{0,30},{2,28},{4,26},{6,24},{8,22},{10,20},{12,18},{14,16},{16,14}... | collective-permute-start | bytes 1474568 | tf_op jit(solution)/shard_map/ppermute | solution.py:331
  417.8 59.6 %collective-permute-start.19 = (f32[2,64,640]{2,1,0:T(8,128)}, f32[2,64,640]{2,1,0:T(8,128)S(1)}, u32[]{:S(2)}, u32[]{:S(2)}) collective-permute-start(f32[2,64,640]{2,1,0:T(8,128)} %get-tuple-element.137), channel_id=1, source_target_pairs={{0,2},{2,0},{4,6},{6,4},{8,10},{10,8},{12,14},{14,12},{16,18},{18,... | collective-permute-start | bytes 983048 | tf_op jit(solution)/shard_map/ppermute | solution.py:331
  453.7 38.9 %collective-permute-start.20 = (f32[2,64,640]{2,1,0:T(8,128)}, f32[2,64,640]{2,1,0:T(8,128)S(1)}, u32[]{:S(2)}, u32[]{:S(2)}) collective-permute-start(f32[2,64,640]{2,1,0:T(8,128)} %get-tuple-element.138), channel_id=1, source_target_pairs={{0,4},{2,6},{4,0},{6,2},{8,12},{10,14},{12,8},{14,10},{16,20},{18,... | collective-permute-start | bytes 983048 | tf_op jit(solution)/shard_map/ppermute | solution.py:331
  495.5 41.3 %collective-permute-start.26 = (f32[2,64,640]{2,1,0:T(8,128)}, f32[2,64,640]{2,1,0:T(8,128)}, u32[]{:S(2)}, u32[]{:S(2)}) collective-permute-start(f32[2,64,640]{2,1,0:T(8,128)} %get-tuple-element.144), channel_id=1, source_target_pairs={{0,16},{2,18},{4,20},{6,22},{8,24},{10,26},{12,28},{14,30},{16,0},... | collective-permute-start | bytes 983048 | tf_op jit(solution)/shard_map/ppermute | solution.py:331
  499.6 39.0 %collective-permute-start.27 = (f32[2,64,640]{2,1,0:T(8,128)}, f32[2,64,640]{2,1,0:T(8,128)}, u32[]{:S(2)}, u32[]{:S(2)}) collective-permute-start(f32[2,64,640]{2,1,0:T(8,128)} %get-tuple-element.145), channel_id=1, source_target_pairs={{0,18},{2,16},{4,22},{6,20},{8,26},{10,24},{12,30},{14,28},{16,2},... | collective-permute-start | bytes 983048 | tf_op jit(solution)/shard_map/ppermute | solution.py:331
  568.9 63.8 %collective-permute-start.59 = (f32[2,32,640]{2,1,0:T(8,128)}, f32[2,32,640]{2,1,0:T(8,128)S(1)}, u32[]{:S(2)}, u32[]{:S(2)}) collective-permute-start(f32[2,32,640]{2,1,0:T(8,128)} %get-tuple-element.184), channel_id=1, source_target_pairs={{0,22},{2,20},{4,18},{6,16},{8,30},{10,28},{12,26},{14,24},{16,6},... | collective-permute-start | bytes 491528 | tf_op jit(solution)/shard_map/ppermute | solution.py:331
  571.3 64.1 %collective-permute-start.60 = (f32[2,32,640]{2,1,0:T(8,128)}, f32[2,32,640]{2,1,0:T(8,128)S(1)}, u32[]{:S(2)}, u32[]{:S(2)}) collective-permute-start(f32[2,32,640]{2,1,0:T(8,128)} %get-tuple-element.185), channel_id=1, source_target_pairs={{0,24},{2,26},{4,28},{6,30},{8,16},{10,18},{12,20},{14,22},{16,8},... | collective-permute-start | bytes 491528 | tf_op jit(solution)/shard_map/ppermute | solution.py:331
  572.6 65.1 %collective-permute-start.61 = (f32[2,32,640]{2,1,0:T(8,128)}, f32[2,32,640]{2,1,0:T(8,128)S(1)}, u32[]{:S(2)}, u32[]{:S(2)}) collective-permute-start(f32[2,32,640]{2,1,0:T(8,128)} %get-tuple-element.186), channel_id=1, source_target_pairs={{0,26},{2,24},{4,30},{6,28},{8,18},{10,16},{12,22},{14,20},{16,10}... | collective-permute-start | bytes 491528 | tf_op jit(solution)/shard_map/ppermute | solution.py:331
  582.1 56.3 %collective-permute-start.62 = (f32[2,32,640]{2,1,0:T(8,128)}, f32[2,32,640]{2,1,0:T(8,128)}, u32[]{:S(2)}, u32[]{:S(2)}) collective-permute-start(f32[2,32,640]{2,1,0:T(8,128)} %get-tuple-element.187), channel_id=1, source_target_pairs={{0,28},{2,30},{4,24},{6,26},{8,20},{10,22},{12,16},{14,18},{16,12}... | collective-permute-start | bytes 491528 | tf_op jit(solution)/shard_map/ppermute | solution.py:331
  585.7 56.9 %collective-permute-start.63 = (f32[2,32,640]{2,1,0:T(8,128)}, f32[2,32,640]{2,1,0:T(8,128)}, u32[]{:S(2)}, u32[]{:S(2)}) collective-permute-start(f32[2,32,640]{2,1,0:T(8,128)} %get-tuple-element.188), channel_id=1, source_target_pairs={{0,30},{2,28},{4,26},{6,24},{8,22},{10,20},{12,18},{14,16},{16,14}... | collective-permute-start | bytes 491528 | tf_op jit(solution)/shard_map/ppermute | solution.py:331
  (106 other events, 4948.2 us)
